TPU v7x, 32 devices: a whole 2x2x4 slice. The times are simulated.
32 devices in a mesh: gx: 8 (over z, y), gy: 4 (over x, core).
Axes of the slice: x: 2, y: 2, z: 4, core: 2. Of those that a mesh axis runs over, the one named last changes fastest.
Arguments:
- section_start: float32 [5, 64, 64, 512], P(None, None, 'gx', 'gy'), may hold values from -2 to 8, as said below
- section_now: float32 [5, 64, 64, 512], P(None, None, 'gx', 'gy'), may hold values from -2 to 8, as said below
- history: bfloat16 [255, 16, 64, 512], P(None, None, 'gx', 'gy'), may hold values from -9 to 9
Outputs:
- section_next: float32 [5, 64, 64, 512], P(None, None, 'gx', 'gy')
- triangle: float32 [256, 256], replicated
Inputs may be any that keep to these rules, and one draw needn't show every extreme that they name: `section_start`: component 0 lies in [1, 2], components 1 to 3 are density times a velocity of magnitude at most 1 in each direction, and component 4 is at least the kinetic energy. `section_now`: as section_start.
All inputs are finite; a program needn't handle non-finite values.
Results may differ from a plain program's by a relative error of at most 0.0003.
Values sent between devices are 32-bit elements; how exact they have to be, the bound alone decides.
No kernel may reach another device: no remote copies, remote signals or barrier semaphores. Data moves between devices by JAX's collectives and lax.ppermute only.
A program may use at most 128 MiB of HBM per device.

v0:
```python
import functools

import jax
import jax.numpy as jnp
from jax import lax
from jax.experimental import pallas as pl
from jax.experimental.pallas import tpu as pltpu
from jax.sharding import PartitionSpec as P


ZSUB = 4
GAMMA_LESS = 0.4
TIME_STEP = 0.2
VISCOUS = 0.25
CHUNK = 8
PIECES = 4


def iota(shape, dim):
    return lax.broadcasted_iota(jnp.int32, shape, dim)


def is_even(axis):
    return lax.rem(lax.axis_index(axis), 2) == 0


def edges_body(now_ref, first_ref, second_ref, cols_ref):
    fields, planes, rows, lanes = now_ref.shape
    even = is_even("gx")
    lo, hi = now_ref[:, :, 0, :], now_ref[:, :, rows - 1, :]
    first_ref[...] = jnp.where(even, hi, lo)
    second_ref[...] = jnp.where(even, lo, hi)
    key = lax.rem((iota((rows, lanes), 1) + 1) // 2, planes)
    masks = 8
    for f in range(fields):
        parts = [jnp.zeros((rows, lanes), jnp.float32)] * masks
        for z in range(planes):
            cells = now_ref[f, z]
            rolled = pltpu.roll(cells, 2 * z, 1) if z else cells
            parts[z % masks] = jnp.where(key == z, rolled, parts[z % masks])
        while len(parts) > 1:
            parts = [x + y for x, y in zip(parts[::2], parts[1::2])]
        cols_ref[f] = parts[0]


def edges(now):
    fields, planes, rows, lanes = now.shape
    assert 2 * planes == lanes
    line = jax.ShapeDtypeStruct((fields, planes, lanes), now.dtype)
    in_vmem = pl.BlockSpec(memory_space=pltpu.VMEM)
    return pl.pallas_call(
        edges_body,
        out_shape=(line, line, jax.ShapeDtypeStruct((fields, rows, lanes), now.dtype)),
        in_specs=[in_vmem],
        out_specs=(in_vmem, in_vmem, in_vmem),
        name="edges",
    )(now)


def state_of(q):
    inverse = 1.0 / q[0]
    speed = [q[k] * inverse for k in (1, 2, 3)]
    twice = q[1] * speed[0] + q[2] * speed[1] + q[3] * speed[2]
    return speed, GAMMA_LESS * (q[4] - 0.5 * twice)


def products_of(q, state):
    speed, pressure = state
    total = q[4] + pressure
    shared = {}
    for i in range(3):
        for j in range(i, 3):
            shared[i, j] = q[1 + i] * speed[j]
    return shared, total


def flux_of(q, state, direction, products=None):
    speed, pressure = state
    shared, total = products or products_of(q, state)
    d = direction - 1
    columns = [q[direction]] + [shared[min(i, d), max(i, d)] for i in range(3)] + [total * speed[d]]
    columns[direction] = columns[direction] + pressure
    return columns


def scaled(q):
    return [2.0 * VISCOUS * x for x in q]


def ahead_of(base, flux):
    return [a - b for a, b in zip(base, flux)]


def behind_of(base, flux):
    return [a + b for a, b in zip(base, flux)]


def only_ahead(q, direction):
    return ahead_of(scaled(q), flux_of(q, state_of(q), direction))


def only_behind(q, direction):
    return behind_of(scaled(q), flux_of(q, state_of(q), direction))


def sides(axis, first, second):
    even = is_even(axis)
    below = [jnp.where(even, b, a) for a, b in zip(first, second)]
    above = [jnp.where(even, a, b) for a, b in zip(first, second)]
    return below, above


def y_halo(first, second):
    left, right = sides("gy", first, second)
    ahead, behind = only_ahead(right, 2), only_behind(left, 2)
    even = iota(ahead[0].shape, 1) % 2 == 0
    return [jnp.where(even, a, pltpu.roll(b, 2, 1)) for a, b in zip(ahead, behind)]


def within_plane(q, base, state, products, edge, x_ahead, x_behind):
    rows, lanes = q[0].shape
    row, lane = iota((rows, lanes), 0), iota((rows, lanes), 1)
    y = flux_of(q, state, 2, products)
    x = flux_of(q, state, 1, products)
    y_a, y_b, x_a, x_b = ahead_of(base, y), behind_of(base, y), ahead_of(base, x), behind_of(base, x)
    sums = []
    for f in range(len(q)):
        part = jnp.where(lane == lanes - 1, edge[f], pltpu.roll(y_a[f], lanes - 1, 1))
        part = part + jnp.where(lane == 0, edge[f], pltpu.roll(y_b[f], 1, 1))
        other = jnp.where(row == rows - 1, x_ahead[f], pltpu.roll(x_a[f], rows - 1, 0))
        other = other + jnp.where(row == 0, x_behind[f], pltpu.roll(x_b[f], 1, 0))
        sums.append(part + other)
    return sums


def advanced(start, now, total):
    return 0.75 * start + (0.25 * (1.0 - 6.0 * VISCOUS * TIME_STEP)) * now + (0.125 * TIME_STEP) * total


def stencil_body(first, *refs):
    now_ref, below_ref, above_ref, start_ref, y_a_ref, y_b_ref, x_a_ref, x_b_ref = refs[:8]
    next_ref, halo_ref = refs[-2:]
    fields, chunk, _, lanes = now_ref.shape
    step = pl.program_id(0)
    base = (first + step) * chunk
    span = range(fields)

    @pl.when(step == 0)
    def _():
        packed = y_halo([y_a_ref[f] for f in span], [y_b_ref[f] for f in span])
        for f in span:
            halo_ref[f] = packed[f]

    x_lo, x_hi = sides("gx", [x_a_ref[f] for f in span], [x_b_ref[f] for f in span])
    x_behind = only_behind(x_lo, 1)
    x_ahead = only_ahead(x_hi, 1)
    turn = lax.rem(lanes - 2 * base, lanes)
    halo = [pltpu.roll(halo_ref[f], turn, 1) for f in span]
    before = only_behind([below_ref[f, 0] for f in span], 3)
    pending = None

    def finish(j, ahead):
        for f in span:
            next_ref[f, j] = advanced(start_ref[f, j], now_ref[f, j], pending[f] + ahead[f])

    for j in range(chunk):
        q = [now_ref[f, j] for f in span]
        state = state_of(q)
        products = products_of(q, state)
        half = scaled(q)
        flux = flux_of(q, state, 3, products)
        if pending is not None:
            finish(j - 1, ahead_of(half, flux))
        edge = [pltpu.roll(halo[f], lanes - 1 - 2 * j, 1) for f in span]
        sums = within_plane(
            q, half, state, products, edge,
            [x_ahead[f][j : j + 1] for f in span], [x_behind[f][j : j + 1] for f in span],
        )
        pending = [sums[f] + before[f] for f in span]
        before = behind_of(half, flux)
    finish(chunk - 1, only_ahead([above_ref[f, 0] for f in span], 3))


def stencil(now, start, around, first, count, into):
    fields, planes, rows, lanes = now.shape
    chunk = CHUNK
    whole = pl.BlockSpec((fields, rows, lanes), lambda c: (0, 0, 0))
    part = pl.BlockSpec((fields, chunk, rows, lanes), lambda c: (0, first + c, 0, 0))
    line = pl.BlockSpec((fields, chunk, lanes), lambda c: (0, first + c, 0))
    below = pl.BlockSpec(
        (fields, 1, rows, lanes), lambda c: (0, jnp.maximum((first + c) * chunk - 1, 0), 0, 0)
    )
    above = pl.BlockSpec(
        (fields, 1, rows, lanes), lambda c: (0, jnp.minimum((first + c + 1) * chunk, planes - 1), 0, 0)
    )
    specs = [part, below, above, part, whole, whole, line, line]
    operands = [now, now, now, start, *around]
    if into is not None:
        specs.append(pl.BlockSpec(memory_space=pl.ANY))
        operands.append(into)
    return pl.pallas_call(
        functools.partial(stencil_body, first),
        out_shape=jax.ShapeDtypeStruct(now.shape, now.dtype),
        grid=(count,),
        in_specs=specs,
        out_specs=part,
        scratch_shapes=[pltpu.VMEM((fields, rows, lanes), jnp.float32)],
        input_output_aliases={} if into is None else {len(operands) - 1: 0},
    )(*operands)


def gram_body(
    older_ref, below_ref, now_ref, above_ref, start_ref, y_a_ref, y_b_ref, x_a_ref, x_b_ref,
    mine_ref, sent_ref, even_ref, odd_ref, total_ref, halo_ref, folded_ref, *, axis,
):
    older, pair, rows, lanes = older_ref.shape
    fields = halo_ref.shape[0]
    snaps = total_ref.shape[0]
    step = pl.program_id(0)
    span = range(fields)

    @pl.when(step == 0)
    def _():
        total_ref[...] = jnp.zeros_like(total_ref)
        odd_ref[...] = jnp.zeros_like(odd_ref)
        packed = y_halo([y_a_ref[f] for f in span], [y_b_ref[f] for f in span])
        for f in span:
            halo_ref[f] = packed[f]

    def parts_of(ref):
        return [ref[pl.ds(r, snaps, stride=rows), :].astype(jnp.bfloat16) for r in range(rows)]

    def newest(which):
        z = ZSUB * (pair * step + which)
        q = [now_ref[f, which, 0] for f in span]
        state = state_of(q)
        products = products_of(q, state)
        half = scaled(q)
        turn = lax.rem(2 * lanes - 1 - 2 * z, lanes)
        edge = [pltpu.roll(halo_ref[f], turn, 1) for f in span]
        x_lo, x_hi = sides(
            "gx", [x_a_ref[f, pl.ds(z, 1), :] for f in span], [x_b_ref[f, pl.ds(z, 1), :] for f in span]
        )
        x_behind, x_ahead = only_behind(x_lo, 1), only_ahead(x_hi, 1)
        sums = within_plane(q, half, state, products, edge, x_ahead, x_behind)
        before = only_behind([below_ref[which][f, 0] for f in span], 3)
        after = only_ahead([above_ref[f, which, 0] for f in span], 3)
        out = [advanced(start_ref[f, which, 0], q[f], sums[f] + before[f] + after[f]) for f in span]
        return state_of(out)[1]

    def fill(ref, which):
        ref[pl.ds(0, older * rows), :] = older_ref[:, which].astype(jnp.float32).reshape(older * rows, lanes)
        ref[pl.ds(older * rows, rows), :] = newest(which)

    def product(parts):
        matrix = jnp.concatenate(parts, axis=1)
        return lax.dot_general(
            matrix, matrix, (((1,), (1,)), ((), ())), preferred_element_type=jnp.float32
        )

    last = parts_of(odd_ref)
    fill(even_ref, 0)
    total_ref[...] += product(last + parts_of(even_ref))
    fill(odd_ref, 1)

    @pl.when(step == pl.num_programs(0) - 1)
    def _():
        total = total_ref[...] + product(parts_of(odd_ref))
        half = snaps // 2
        first, final = total[:half, :half], total[half:, half:]
        r, c = iota((half, half), 0), iota((half, half), 1)
        folded_ref[:half] = jnp.where(r <= c, first, final)
        folded_ref[half : 2 * half] = total[:half, half:]
        diagonal = jnp.sum(jnp.where(r == c, final, 0.0), axis=0, keepdims=True)
        folded_ref[2 * half :] = jnp.broadcast_to(diagonal, (folded_ref.shape[0] - 2 * half, half))
        size = mine_ref.shape[0]
        side = lax.rem(lax.axis_index(axis), 2)
        mine_ref[...] = folded_ref[pl.ds(pl.multiple_of(side * size, 8), size), :]
        sent_ref[...] = folded_ref[pl.ds(pl.multiple_of((1 - side) * size, 8), size), :]


def gram(history, now, start, around, axis):
    older, samples, rows, lanes = history.shape
    fields, planes = now.shape[:2]
    snaps = older + 1
    half = snaps // 2
    pair = 2
    size = half + 8
    grouped = (fields, samples, ZSUB, rows, lanes)

    def below(which):
        return pl.BlockSpec(
            (fields, 1, rows, lanes),
            lambda p: (0, jnp.maximum(ZSUB * (pair * p + which) - 1, 0), 0, 0),
        )

    def plane(offset):
        return pl.BlockSpec((fields, pair, 1, rows, lanes), lambda p: (0, p, offset, 0, 0))

    whole = pl.BlockSpec((fields, rows, lanes), lambda p: (0, 0, 0))
    line = pl.BlockSpec((fields, planes, lanes), lambda p: (0, 0, 0))
    result = pl.BlockSpec((size, half), lambda p: (0, 0))

    def body(older_ref, below_0, below_1, *refs):
        gram_body(older_ref, (below_0, below_1), *refs, axis=axis)

    return pl.pallas_call(
        body,
        out_shape=(jax.ShapeDtypeStruct((size, half), jnp.float32),) * 2,
        grid=(samples // pair,),
        in_specs=[
            pl.BlockSpec((older, pair, rows, lanes), lambda p: (0, p, 0, 0)),
            below(0), below(1), plane(0), plane(1), plane(0), whole, whole, line, line,
        ],
        out_specs=(result, result),
        scratch_shapes=[
            pltpu.VMEM((snaps * rows, lanes), jnp.float32),
            pltpu.VMEM((snaps * rows, lanes), jnp.float32),
            pltpu.VMEM((snaps, snaps), jnp.float32),
            pltpu.VMEM((fields, rows, lanes), jnp.float32),
            pltpu.VMEM((2 * size, half), jnp.float32),
        ],
        name="gram",
    )(
        history, now, now, now.reshape(grouped), now.reshape(grouped), start.reshape(grouped), *around
    )


def factor_body(scale, axis, mine_ref, other_ref, out_ref, gram_ref, folded_ref):
    size, half = mine_ref.shape
    side = lax.rem(lax.axis_index(axis), 2)
    folded_ref[pl.ds(pl.multiple_of(side * size, 8), size), :] = mine_ref[...]
    folded_ref[pl.ds(pl.multiple_of((1 - side) * size, 8), size), :] = other_ref[...]
    group = 8
    r, c = iota((half, half), 0), iota((half, half), 1)
    mixed = folded_ref[:half] * scale
    turned = mixed.T
    gram_ref[:half, :half] = jnp.where(r <= c, mixed, turned)
    gram_ref[:half, half:] = folded_ref[half : 2 * half] * scale
    diagonal = jnp.broadcast_to(folded_ref[2 * half : 2 * half + 1] * scale, (half, half))
    gram_ref[half:, half:] = jnp.where(r == c, diagonal, jnp.where(r > c, mixed, turned))
    out_ref[half:, :half] = jnp.zeros((half, half), jnp.float32)
    sub, lane = iota((group, half), 0), iota((group, half), 1)
    span = range(group)

    def column(x, index):
        return jnp.broadcast_to(x[:, index : index + 1], (group, half))

    def line(x, index):
        return jnp.broadcast_to(x[index : index + 1, :], (group, half))

    per = half // group
    for panel in range(2):
        width = 2 - panel
        tiles = [
            [
                gram_ref[pl.ds(panel * half + group * t, group), pl.ds((panel + v) * half, half)]
                for v in range(width)
            ]
            for t in range(per)
        ]
        for t in range(per):
            first = group * t
            own = [column(tiles[t][0], first + j) for j in span]
            pivot = {(i, j): line(own[j], i) for j in span for i in range(j + 1)}
            rows = [[line(x, i) for x in tiles[t]] for i in span]
            later = range(t + 1, per)
            lower = {m: [column(tiles[m][0], first + j) for j in span] for m in later}
            for i in span:
                inverse = lax.rsqrt(pivot[i, i])
                for j in range(i + 1, group):
                    pivot[i, j] = pivot[i, j] * inverse
                for j in range(i + 1, group):
                    for k in range(j, group):
                        pivot[j, k] = pivot[j, k] - pivot[i, j] * pivot[i, k]
                rows[i] = [x * inverse for x in rows[i]]
                for j in range(i + 1, group):
                    rows[j] = [a - pivot[i, j] * b for a, b in zip(rows[j], rows[i])]
                for m in later:
                    entry = lower[m][i] * inverse
                    for j in range(i + 1, group):
                        lower[m][j] = lower[m][j] - entry * pivot[i, j]
                    tiles[m] = [a - entry * b for a, b in zip(tiles[m], rows[i])]
            for v in range(width):
                merged = rows[0][v]
                for i in range(1, group):
                    merged = jnp.where(sub == i, rows[i][v], merged)
                if v == 0:
                    merged = jnp.where(lane >= first + sub, merged, 0.0)
                out_ref[pl.ds(panel * half + first, group), pl.ds((panel + v) * half, half)] = merged
        if panel == 0:
            across = out_ref[:half, half:]
            gram_ref[half:, half:] = gram_ref[half:, half:] - lax.dot_general(
                across,
                across,
                (((0,), (0,)), ((), ())),
                precision=lax.Precision.HIGHEST,
                preferred_element_type=jnp.float32,
            )


def factor(mine, other, rows_total, axis):
    size, half = mine.shape
    in_vmem = pl.BlockSpec(memory_space=pltpu.VMEM)
    return pl.pallas_call(
        functools.partial(factor_body, 1.0 / rows_total, axis),
        out_shape=jax.ShapeDtypeStruct((2 * half, 2 * half), jnp.float32),
        in_specs=[in_vmem, in_vmem],
        out_specs=in_vmem,
        scratch_shapes=[
            pltpu.VMEM((2 * half, 2 * half), jnp.float32),
            pltpu.VMEM((2 * size, half), jnp.float32),
        ],
        name="factor",
    )(mine, other)


def local(section_start, section_now, history):
    axes = ("gx", "gy")
    count = lax.axis_size("gx") * lax.axis_size("gy")
    first, second, cols = edges(section_now)

    def neighbours(part, axis, by):
        size = lax.axis_size(axis)
        assert size % 2 == 0
        return lax.ppermute(part, axis, [(i, (i + by * (-1) ** i) % size) for i in range(size)])

    def swap(part, bit):
        return lax.ppermute(part, axes, [(i, i ^ bit) for i in range(count)])

    x_a, x_b = neighbours(first, "gx", 1), neighbours(second, "gx", -1)
    y_a, y_b = neighbours(cols, "gy", 1), neighbours(cols, "gy", -1)
    around = (y_a, y_b, x_a, x_b)
    mine, sent = gram(history, section_now, section_start, around, "gy")
    mine = mine + swap(sent, 1)
    bit = 2
    while bit < count:
        mine = mine + swap(mine, bit)
        bit *= 2
    rows_total = history[0].size * count
    triangle = factor(mine, swap(mine, 1), rows_total, "gy")
    chunks = section_now.shape[1] // CHUNK
    section_next = None
    for piece in range(PIECES):
        low, high = piece * chunks // PIECES, (piece + 1) * chunks // PIECES
        section_next = stencil(section_now, section_start, around, low, high - low, section_next)
    return (section_next, triangle)


def solution(mesh):
    placed = P(None, None, "gx", "gy")
    return jax.shard_map(
        local,
        mesh=mesh,
        in_specs=(placed, placed, placed),
        out_specs=(placed, P()),
        check_vma=False,
    )
```

profile of v0, /device:TPU:0, one launch (start us, length us, event | category | flops | bytes accessed | tf_op | source)
XLA Modules:
  0.0 67.7 jit_solution(4849829379344806166)
XLA Ops:
  0.6 2.9 %edges.1 = (f32[5,64,128]{2,1,0:T(8,128)}, f32[5,64,128]{2,1,0:T(8,128)}, f32[5,8,128]{2,1,0:T(8,128)}) custom-call(f32[5,64,8,128]{3,2,1,0:T(8,128)} %below_1.1), custom_call_target="tpu_custom_call" | custom-call | tf_op jit(solution)/shard_map/edges/pallas_call | solution.py:51
  3.5 3.0 %collective-permute-start.2 = (f32[5,64,128]{2,1,0:T(8,128)}, f32[5,64,128]{2,1,0:T(8,128)S(1)}, u32[]{:S(2)}, u32[]{:S(2)}) collective-permute-start(f32[5,64,128]{2,1,0:T(8,128)} %get-tuple-element.8), channel_id=1, source_target_pairs={{0,4},{4,0},{8,12},{12,8},{16,20},{20,16},{24,28},{28,24},{1,5},{5... | collective-permute-start | bytes 491528 | tf_op jit(solution)/shard_map/ppermute | solution.py:426
  6.5 3.5 %collective-permute-start.3 = (f32[5,64,128]{2,1,0:T(8,128)}, f32[5,64,128]{2,1,0:T(8,128)S(1)}, u32[]{:S(2)}, u32[]{:S(2)}) collective-permute-start(f32[5,64,128]{2,1,0:T(8,128)} %get-tuple-element.9), channel_id=1, source_target_pairs={{0,28},{4,8},{8,4},{12,16},{16,12},{20,24},{24,20},{28,0},{1,29},{... | collective-permute-start | bytes 491528 | tf_op jit(solution)/shard_map/ppermute | solution.py:426
  10.1 1.6 %collective-permute-start.1 = (f32[5,8,128]{2,1,0:T(8,128)}, f32[5,8,128]{2,1,0:T(8,128)S(1)}, u32[]{:S(2)}, u32[]{:S(2)}) collective-permute-start(f32[5,8,128]{2,1,0:T(8,128)} %get-tuple-element.7), channel_id=1, source_target_pairs={{0,3},{1,2},{2,1},{3,0},{4,7},{5,6},{6,5},{7,4},{8,11},{9,10},{10,... | collective-permute-start | bytes 61448 | tf_op jit(solution)/shard_map/ppermute | solution.py:426
  11.7 1.8 %collective-permute-done.1.refs_5_.refs_4_ = f32[5,8,128]{2,1,0:T(8,128)S(1)} collective-permute-done((f32[5,8,128]{2,1,0:T(8,128)}, f32[5,8,128]{2,1,0:T(8,128)S(1)}, u32[]{:S(2)}, u32[]{:S(2)}) %collective-permute-start.1) | collective-permute-done | bytes 20512 | tf_op jit(solution)/shard_map/ppermute | solution.py:426
  13.8 1.3 %collective-permute-done.3.refs_7_.refs_6_ = f32[5,64,128]{2,1,0:T(8,128)S(1)} collective-permute-done((f32[5,64,128]{2,1,0:T(8,128)}, f32[5,64,128]{2,1,0:T(8,128)S(1)}, u32[]{:S(2)}, u32[]{:S(2)}) %collective-permute-start.3) | collective-permute-done | bytes 163872 | tf_op jit(solution)/shard_map/ppermute | solution.py:426
  15.1 0.7 copy-done.1
  15.8 10.3 %gram.1 = (f32[136,128]{1,0:T(8,128)}, f32[136,128]{1,0:T(8,128)}) custom-call(bf16[255,16,8,128]{3,2,1,0:T(8,128)(2,1)} %older_ref.1, f32[5,64,8,128]{3,2,1,0:T(8,128)} %below_1.1, f32[5,64,8,128]{3,2,1,0:T(8,128)} %below_1.1, f32[5,16,4,8,128]{4,3,2,1,0:T(8,128)} %bitcast.2, f32[5,16,4,8,128]{4,3,2,1,0:T(8,128)} %bitcast.3, f32[5,16,4,8,128]{4,3,2,1,0:T(8,128)} %bitcast.4, ...), custom_call_target="tpu_custom_call" | custom-call | tf_op jit(solution)/shard_map/gram/pallas_call | solution.py:307
  26.1 1.5 %collective-permute-done.4 = f32[136,128]{1,0:T(8,128)S(1)} collective-permute-done((f32[136,128]{1,0:T(8,128)}, f32[136,128]{1,0:T(8,128)S(1)}, u32[]{:S(2)}, u32[]{:S(2)}) %collective-permute-start.4) | collective-permute-done | bytes 69664 | tf_op jit(solution)/shard_map/ppermute | solution.py:429
  27.5 0.9 %add.15 = f32[136,128]{1,0:T(8,128)S(1)} add(f32[136,128]{1,0:T(8,128)} %get-tuple-element.10, f32[136,128]{1,0:T(8,128)S(1)} %collective-permute-done.4) | non-fusion elementwise | flops 17408 | bytes 208896 | tf_op jit(solution)/shard_map/add | solution.py:435
  28.4 1.6 %collective-permute-start.5 = (f32[136,128]{1,0:T(8,128)S(1)}, f32[136,128]{1,0:T(8,128)S(1)}, u32[]{:S(2)}, u32[]{:S(2)}) collective-permute-start(f32[136,128]{1,0:T(8,128)S(1)} %add.15), channel_id=1, source_target_pairs={{0,2},{1,3},{2,0},{3,1},{4,6},{5,7},{6,4},{7,5},{8,10},{9,11},{10,... | collective-permute-start | bytes 208904 | tf_op jit(solution)/shard_map/ppermute | solution.py:429
  30.0 2.8 %collective-permute-done.5 = f32[136,128]{1,0:T(8,128)S(1)} collective-permute-done((f32[136,128]{1,0:T(8,128)S(1)}, f32[136,128]{1,0:T(8,128)S(1)}, u32[]{:S(2)}, u32[]{:S(2)}) %collective-permute-start.5) | collective-permute-done | bytes 69664 | tf_op jit(solution)/shard_map/ppermute | solution.py:429
  32.8 1.2 %collective-permute-start.6 = (f32[136,128]{1,0:T(8,128)S(1)}, f32[136,128]{1,0:T(8,128)S(1)}, u32[]{:S(2)}, u32[]{:S(2)}) collective-permute-start(f32[136,128]{1,0:T(8,128)S(1)} %add.16), channel_id=1, source_target_pairs={{0,4},{1,5},{2,6},{3,7},{4,0},{5,1},{6,2},{7,3},{8,12},{9,13},{10,... | collective-permute-start | bytes 208904 | tf_op jit(solution)/shard_map/ppermute | solution.py:429
  34.0 3.2 %collective-permute-done.6 = f32[136,128]{1,0:T(8,128)S(1)} collective-permute-done((f32[136,128]{1,0:T(8,128)S(1)}, f32[136,128]{1,0:T(8,128)S(1)}, u32[]{:S(2)}, u32[]{:S(2)}) %collective-permute-start.6) | collective-permute-done | bytes 69664 | tf_op jit(solution)/shard_map/ppermute | solution.py:429
  37.2 1.3 %collective-permute-start.7 = (f32[136,128]{1,0:T(8,128)S(1)}, f32[136,128]{1,0:T(8,128)S(1)}, u32[]{:S(2)}, u32[]{:S(2)}) collective-permute-start(f32[136,128]{1,0:T(8,128)S(1)} %add.17), channel_id=1, source_target_pairs={{0,8},{1,9},{2,10},{3,11},{4,12},{5,13},{6,14},{7,15},{8,0},{9,1},... | collective-permute-start | bytes 208904 | tf_op jit(solution)/shard_map/ppermute | solution.py:429
  38.5 3.1 %collective-permute-done.7 = f32[136,128]{1,0:T(8,128)S(1)} collective-permute-done((f32[136,128]{1,0:T(8,128)S(1)}, f32[136,128]{1,0:T(8,128)S(1)}, u32[]{:S(2)}, u32[]{:S(2)}) %collective-permute-start.7) | collective-permute-done | bytes 69664 | tf_op jit(solution)/shard_map/ppermute | solution.py:429
  41.6 3.0 %collective-permute-start.8 = (f32[136,128]{1,0:T(8,128)S(1)}, f32[136,128]{1,0:T(8,128)S(1)}, u32[]{:S(2)}, u32[]{:S(2)}) collective-permute-start(f32[136,128]{1,0:T(8,128)S(1)} %add.18), channel_id=1, source_target_pairs={{0,16},{1,17},{2,18},{3,19},{4,20},{5,21},{6,22},{7,23},{8,24},{9,... | collective-permute-start | bytes 208904 | tf_op jit(solution)/shard_map/ppermute | solution.py:429
  44.6 3.0 %collective-permute-done.8 = f32[136,128]{1,0:T(8,128)S(1)} collective-permute-done((f32[136,128]{1,0:T(8,128)S(1)}, f32[136,128]{1,0:T(8,128)S(1)}, u32[]{:S(2)}, u32[]{:S(2)}) %collective-permute-start.8) | collective-permute-done | bytes 69664 | tf_op jit(solution)/shard_map/ppermute | solution.py:429
  47.8 2.4 %shard_map.50.refs_8_ = f32[5,64,8,128]{3,2,1,0:T(8,128)} custom-call(f32[5,64,8,128]{3,2,1,0:T(8,128)} %below_1.1, f32[5,64,8,128]{3,2,1,0:T(8,128)} %below_1.1, f32[5,64,8,128]{3,2,1,0:T(8,128)} %below_1.1, f32[5,64,8,128]{3,2,1,0:T(8,128)} %refs_3_.7, f32[5,8,128]{2,1,0:T(8,128)} %copy-done.2, f32[5,8,128]{2,1,0:T(8,128)} %copy-done.3, ...), custom_call_target="tpu_custom_call" | custom-call | tf_op jit(solution)/shard_map/pallas_call | solution.py:201
  50.2 2.4 %shard_map.51.refs_8_ = f32[5,64,8,128]{3,2,1,0:T(8,128)} custom-call(f32[5,64,8,128]{3,2,1,0:T(8,128)} %below_1.1, f32[5,64,8,128]{3,2,1,0:T(8,128)} %below_1.1, f32[5,64,8,128]{3,2,1,0:T(8,128)} %below_1.1, f32[5,64,8,128]{3,2,1,0:T(8,128)} %refs_3_.7, f32[5,8,128]{2,1,0:T(8,128)} %copy-done.2, ...), custom_call_target="tpu_custom_call", output_to_operand_aliasing={{}: (8, {})} | custom-call | tf_op jit(solution)/shard_map/pallas_call | solution.py:201
  52.6 2.4 %shard_map.52.refs_8_ = f32[5,64,8,128]{3,2,1,0:T(8,128)} custom-call(f32[5,64,8,128]{3,2,1,0:T(8,128)} %below_1.1, f32[5,64,8,128]{3,2,1,0:T(8,128)} %below_1.1, f32[5,64,8,128]{3,2,1,0:T(8,128)} %below_1.1, f32[5,64,8,128]{3,2,1,0:T(8,128)} %refs_3_.7, f32[5,8,128]{2,1,0:T(8,128)} %copy-done.2, ...), custom_call_target="tpu_custom_call", output_to_operand_aliasing={{}: (8, {})} | custom-call | tf_op jit(solution)/shard_map/pallas_call | solution.py:201
  55.1 2.4 %shard_map.53 = f32[5,64,8,128]{3,2,1,0:T(8,128)} custom-call(f32[5,64,8,128]{3,2,1,0:T(8,128)} %below_1.1, f32[5,64,8,128]{3,2,1,0:T(8,128)} %below_1.1, f32[5,64,8,128]{3,2,1,0:T(8,128)} %below_1.1, f32[5,64,8,128]{3,2,1,0:T(8,128)} %refs_3_.7, f32[5,8,128]{2,1,0:T(8,128)} %copy-done.2, f32[5,8,128]{2,1,0:T(8,128)} %copy-done.3, ...), custom_call_target="tpu_custom_call", output_to_operand_aliasing={{}: (8, {})} | custom-call | tf_op jit(solution)/shard_map/pallas_call | solution.py:201
  57.5 0.6 copy-done.5
  58.1 9.5 %factor.1 = f32[256,256]{1,0:T(8,128)} custom-call(f32[136,128]{1,0:T(8,128)} %copy-done.4, f32[136,128]{1,0:T(8,128)} %copy-done.5), custom_call_target="tpu_custom_call" | custom-call | tf_op jit(solution)/shard_map/factor/pallas_call | solution.py:405
  (20 shorter events, 0.5 us)
Async XLA Ops:
  3.5 10.3 %collective-permute-start.2 = (f32[5,64,128]{2,1,0:T(8,128)}, f32[5,64,128]{2,1,0:T(8,128)S(1)}, u32[]{:S(2)}, u32[]{:S(2)}) collective-permute-start(f32[5,64,128]{2,1,0:T(8,128)} %get-tuple-element.8), channel_id=1, source_target_pairs={{0,4},{4,0},{8,12},{12,8},{16,20},{20,16},{24,28},{28,24},{1,5},{5... | collective-permute-start | bytes 491528 | tf_op jit(solution)/shard_map/ppermute | solution.py:426
  6.5 8.6 %collective-permute-start.3 = (f32[5,64,128]{2,1,0:T(8,128)}, f32[5,64,128]{2,1,0:T(8,128)S(1)}, u32[]{:S(2)}, u32[]{:S(2)}) collective-permute-start(f32[5,64,128]{2,1,0:T(8,128)} %get-tuple-element.9), channel_id=1, source_target_pairs={{0,28},{4,8},{8,4},{12,16},{16,12},{20,24},{24,20},{28,0},{1,29},{... | collective-permute-start | bytes 491528 | tf_op jit(solution)/shard_map/ppermute | solution.py:426
  10.1 1.6 %collective-permute-start = (f32[5,8,128]{2,1,0:T(8,128)}, f32[5,8,128]{2,1,0:T(8,128)S(1)}, u32[]{:S(2)}, u32[]{:S(2)}) collective-permute-start(f32[5,8,128]{2,1,0:T(8,128)} %get-tuple-element.7), channel_id=1, source_target_pairs={{0,1},{1,0},{2,3},{3,2},{4,5},{5,4},{6,7},{7,6},{8,9},{9,8},{10,11... | collective-permute-start | bytes 61448 | tf_op jit(solution)/shard_map/ppermute | solution.py:426
  10.1 3.4 %collective-permute-start.1 = (f32[5,8,128]{2,1,0:T(8,128)}, f32[5,8,128]{2,1,0:T(8,128)S(1)}, u32[]{:S(2)}, u32[]{:S(2)}) collective-permute-start(f32[5,8,128]{2,1,0:T(8,128)} %get-tuple-element.7), channel_id=1, source_target_pairs={{0,3},{1,2},{2,1},{3,0},{4,7},{5,6},{6,5},{7,4},{8,11},{9,10},{10,... | collective-permute-start | bytes 61448 | tf_op jit(solution)/shard_map/ppermute | solution.py:426
  11.7 3.4 %copy-start.2 = (f32[5,8,128]{2,1,0:T(8,128)}, f32[5,8,128]{2,1,0:T(8,128)S(1)}, u32[]{:S(2)}) copy-start(f32[5,8,128]{2,1,0:T(8,128)S(1)} %collective-permute-done.refs_4_.refs_3_) | copy-start | bytes 61444
  13.5 1.6 %copy-start.3 = (f32[5,8,128]{2,1,0:T(8,128)}, f32[5,8,128]{2,1,0:T(8,128)S(1)}, u32[]{:S(2)}) copy-start(f32[5,8,128]{2,1,0:T(8,128)S(1)} %collective-permute-done.1.refs_5_.refs_4_) | copy-start | bytes 61444
  13.8 1.3 %copy-start = (f32[5,64,128]{2,1,0:T(8,128)}, f32[5,64,128]{2,1,0:T(8,128)S(1)}, u32[]{:S(2)}) copy-start(f32[5,64,128]{2,1,0:T(8,128)S(1)} %collective-permute-done.2.refs_6_.refs_5_) | copy-start | bytes 491524
  15.1 0.7 copy-start.1
  26.1 1.5 %collective-permute-start.4 = (f32[136,128]{1,0:T(8,128)}, f32[136,128]{1,0:T(8,128)S(1)}, u32[]{:S(2)}, u32[]{:S(2)}) collective-permute-start(f32[136,128]{1,0:T(8,128)} %get-tuple-element.11), channel_id=1, source_target_pairs={{0,1},{1,0},{2,3},{3,2},{4,5},{5,4},{6,7},{7,6},{8,9},{9,8},{10,11... | collective-permute-start | bytes 208904 | tf_op jit(solution)/shard_map/ppermute | solution.py:429
  28.4 4.4 %collective-permute-start.5 = (f32[136,128]{1,0:T(8,128)S(1)}, f32[136,128]{1,0:T(8,128)S(1)}, u32[]{:S(2)}, u32[]{:S(2)}) collective-permute-start(f32[136,128]{1,0:T(8,128)S(1)} %add.15), channel_id=1, source_target_pairs={{0,2},{1,3},{2,0},{3,1},{4,6},{5,7},{6,4},{7,5},{8,10},{9,11},{10,... | collective-permute-start | bytes 208904 | tf_op jit(solution)/shard_map/ppermute | solution.py:429
  32.8 4.4 %collective-permute-start.6 = (f32[136,128]{1,0:T(8,128)S(1)}, f32[136,128]{1,0:T(8,128)S(1)}, u32[]{:S(2)}, u32[]{:S(2)}) collective-permute-start(f32[136,128]{1,0:T(8,128)S(1)} %add.16), channel_id=1, source_target_pairs={{0,4},{1,5},{2,6},{3,7},{4,0},{5,1},{6,2},{7,3},{8,12},{9,13},{10,... | collective-permute-start | bytes 208904 | tf_op jit(solution)/shard_map/ppermute | solution.py:429
  37.2 4.4 %collective-permute-start.7 = (f32[136,128]{1,0:T(8,128)S(1)}, f32[136,128]{1,0:T(8,128)S(1)}, u32[]{:S(2)}, u32[]{:S(2)}) collective-permute-start(f32[136,128]{1,0:T(8,128)S(1)} %add.17), channel_id=1, source_target_pairs={{0,8},{1,9},{2,10},{3,11},{4,12},{5,13},{6,14},{7,15},{8,0},{9,1},... | collective-permute-start | bytes 208904 | tf_op jit(solution)/shard_map/ppermute | solution.py:429
  41.6 6.0 %collective-permute-start.8 = (f32[136,128]{1,0:T(8,128)S(1)}, f32[136,128]{1,0:T(8,128)S(1)}, u32[]{:S(2)}, u32[]{:S(2)}) collective-permute-start(f32[136,128]{1,0:T(8,128)S(1)} %add.18), channel_id=1, source_target_pairs={{0,16},{1,17},{2,18},{3,19},{4,20},{5,21},{6,22},{7,23},{8,24},{9,... | collective-permute-start | bytes 208904 | tf_op jit(solution)/shard_map/ppermute | solution.py:429
  47.7 2.5 %copy-start.4 = (f32[136,128]{1,0:T(8,128)}, f32[136,128]{1,0:T(8,128)S(1)}, u32[]{:S(2)}) copy-start(f32[136,128]{1,0:T(8,128)S(1)} %add.19.mine_ref) | copy-start | bytes 208900
  47.7 9.8 %collective-permute-start.9 = (f32[136,128]{1,0:T(8,128)S(1)}, f32[136,128]{1,0:T(8,128)S(1)}, u32[]{:S(2)}, u32[]{:S(2)}) collective-permute-start(f32[136,128]{1,0:T(8,128)S(1)} %add.19.mine_ref), channel_id=1, source_target_pairs={{0,1},{1,0},{2,3},{3,2},{4,5},{5,4},{6,7},{7,6},{8,9},{9,8},{10,11... | collective-permute-start | bytes 208904 | tf_op jit(solution)/shard_map/ppermute | solution.py:429
  57.5 0.6 copy-start.5
where the time goes:
time: 68.1 us; the launch traced here: 67.7 us
  Pallas kernels  32.5 us (48%)
  waiting for transfers between devices  17 us (25%)
  starting transfers between devices  15.3 us (22%)
  local copies, waits for them, and re-layouts  1.3 us (2%)
  other arithmetic  0.93 us (1%)
  between operations  0.7 us (1%)
    ppermute x6, waiting for transfers between devices, swap(): return lax.ppermute(part, axes, [(i, i ^ bit) for i in range(count)])  13.6 us
    pallas_call x1, Pallas kernels, gram(): pl.pallas_call(body, out_shape=(jax.ShapeDtypeStruct((size, half), jnp.fl...  10.3 us
    pallas_call x4, Pallas kernels, stencil(): pl.pallas_call(functools.partial(stencil_body, first), out_shape=jax.Shap...  9.74 us
    pallas_call x1, Pallas kernels, factor(): pl.pallas_call(functools.partial(factor_body, 1.0 / rows_total, axis), ou...  9.52 us
    ppermute x4, starting transfers between devices, neighbours(): lax.ppermute(part, axis, [(i, (i + by * (-1) ** i) % size) for i in range...  8.15 us
    ppermute x6, starting transfers between devices, swap(): return lax.ppermute(part, axes, [(i, i ^ bit) for i in range(count)])  7.12 us
    ppermute x4, waiting for transfers between devices, neighbours(): lax.ppermute(part, axis, [(i, (i + by * (-1) ** i) % size) for i in range...  3.41 us
    pallas_call x1, Pallas kernels, edges(): pl.pallas_call(edges_body, out_shape=(line, line, jax.ShapeDtypeStruct((f...  2.92 us
  transfers between devices with their start and end apart: 10, of which 8 were waited for; matrix products, arithmetic and copies ran while one was open for 0% of the time, Pallas kernels for 14%

commit v1 on v0

--- a/solution.py
+++ b/solution.py
@@ -209,29 +209,72 @@
     )(*operands)
 
 
+def relayout_body(older_ref, out_ref, *cells_refs):
+    older, _, rows, lanes = older_ref.shape
+    snaps = out_ref.shape[1]
+
+    @pl.when(pl.program_id(0) == 0)
+    def _():
+        for ref in cells_refs:
+            ref[pl.ds(older * rows, (snaps - older) * rows), :] = jnp.zeros(
+                ((snaps - older) * rows, lanes), jnp.float32
+            )
+
+    for which, ref in enumerate(cells_refs):
+        ref[pl.ds(0, older * rows), :] = older_ref[:, which].astype(jnp.float32).reshape(older * rows, lanes)
+    for which, ref in enumerate(cells_refs):
+        for r in range(rows):
+            part = ref[pl.ds(r, snaps, stride=rows), :]
+            out_ref[which, :, r * lanes : (r + 1) * lanes] = part.astype(out_ref.dtype)
+
+
+def relayout(history):
+    older, samples, rows, lanes = history.shape
+    snaps = older + 1
+    pair = 2
+    return pl.pallas_call(
+        relayout_body,
+        out_shape=jax.ShapeDtypeStruct((samples, snaps, rows * lanes), history.dtype),
+        grid=(samples // pair,),
+        in_specs=[pl.BlockSpec((older, pair, rows, lanes), lambda p: (0, p, 0, 0))],
+        out_specs=pl.BlockSpec((pair, snaps, rows * lanes), lambda p: (p, 0, 0)),
+        scratch_shapes=[pltpu.VMEM((snaps * rows, lanes), jnp.float32)] * pair,
+        name="relayout",
+    )(history)
+
+
 def gram_body(
-    older_ref, below_ref, now_ref, above_ref, start_ref, y_a_ref, y_b_ref, x_a_ref, x_b_ref,
-    mine_ref, sent_ref, even_ref, odd_ref, total_ref, halo_ref, folded_ref, *, axis,
+    cells_ref, below_refs, now_ref, above_ref, start_ref, y_a_ref, y_b_ref, x_a_ref, x_b_ref,
+    mine_ref, sent_ref, newest_ref, total_ref, halo_ref, folded_ref, *, axis,
 ):
-    older, pair, rows, lanes = older_ref.shape
-    fields = halo_ref.shape[0]
-    snaps = total_ref.shape[0]
+    pair, snaps, width = cells_ref.shape
+    fields, rows, lanes = halo_ref.shape
     step = pl.program_id(0)
+    groups = pl.num_programs(0) - 1
     span = range(fields)
+    tile = 16
 
     @pl.when(step == 0)
     def _():
-        total_ref[...] = jnp.zeros_like(total_ref)
-        odd_ref[...] = jnp.zeros_like(odd_ref)
+        newest_ref[...] = jnp.zeros_like(newest_ref)
         packed = y_halo([y_a_ref[f] for f in span], [y_b_ref[f] for f in span])
         for f in span:
             halo_ref[f] = packed[f]
 
-    def parts_of(ref):
-        return [ref[pl.ds(r, snaps, stride=rows), :].astype(jnp.bfloat16) for r in range(rows)]
+    bottom = iota((tile, width), 0) == tile - 1
+    parts = []
+    for which in range(pair):
+        row = jnp.concatenate([newest_ref[which, r : r + 1, :] for r in range(rows)], axis=1)
+        last = cells_ref[which, snaps - tile :, :].astype(jnp.float32)
+        last = jnp.where(bottom, row, last).astype(cells_ref.dtype)
+        parts.append(jnp.concatenate([cells_ref[which, : snaps - tile, :], last], axis=0))
+    matrix = jnp.concatenate(parts, axis=1)
+    product = lax.dot_general(
+        matrix, matrix, (((1,), (1,)), ((), ())), preferred_element_type=jnp.float32
+    )
 
     def newest(which):
-        z = ZSUB * (pair * step + which)
+        z = ZSUB * (pair * jnp.minimum(step, groups - 1) + which)
         q = [now_ref[f, which, 0] for f in span]
         state = state_of(q)
         products = products_of(q, state)
@@ -243,34 +286,23 @@
         )
         x_behind, x_ahead = only_behind(x_lo, 1), only_ahead(x_hi, 1)
         sums = within_plane(q, half, state, products, edge, x_ahead, x_behind)
-        before = only_behind([below_ref[which][f, 0] for f in span], 3)
+        before = only_behind([below_refs[which][f, 0] for f in span], 3)
         after = only_ahead([above_ref[f, which, 0] for f in span], 3)
         out = [advanced(start_ref[f, which, 0], q[f], sums[f] + before[f] + after[f]) for f in span]
         return state_of(out)[1]
 
-    def fill(ref, which):
-        ref[pl.ds(0, older * rows), :] = older_ref[:, which].astype(jnp.float32).reshape(older * rows, lanes)
-        ref[pl.ds(older * rows, rows), :] = newest(which)
-
-    def product(parts):
-        matrix = jnp.concatenate(parts, axis=1)
-        return lax.dot_general(
-            matrix, matrix, (((1,), (1,)), ((), ())), preferred_element_type=jnp.float32
-        )
-
-    last = parts_of(odd_ref)
-    fill(even_ref, 0)
-    total_ref[...] += product(last + parts_of(even_ref))
-    fill(odd_ref, 1)
-
-    @pl.when(step == pl.num_programs(0) - 1)
+    fresh = [newest(which) for which in range(pair)]
+    for which in range(pair):
+        newest_ref[which] = fresh[which]
+    total_ref[...] = jnp.where(step > 1, total_ref[...], 0.0) + product
+
+    @pl.when(step == groups)
     def _():
-        total = total_ref[...] + product(parts_of(odd_ref))
         half = snaps // 2
-        first, final = total[:half, :half], total[half:, half:]
+        first, final = total_ref[:half, :half], total_ref[half:, half:]
         r, c = iota((half, half), 0), iota((half, half), 1)
         folded_ref[:half] = jnp.where(r <= c, first, final)
-        folded_ref[half : 2 * half] = total[:half, half:]
+        folded_ref[half : 2 * half] = total_ref[:half, half:]
         diagonal = jnp.sum(jnp.where(r == c, final, 0.0), axis=0, keepdims=True)
         folded_ref[2 * half :] = jnp.broadcast_to(diagonal, (folded_ref.shape[0] - 2 * half, half))
         size = mine_ref.shape[0]
@@ -279,50 +311,51 @@
         sent_ref[...] = folded_ref[pl.ds(pl.multiple_of((1 - side) * size, 8), size), :]
 
 
-def gram(history, now, start, around, axis):
-    older, samples, rows, lanes = history.shape
-    fields, planes = now.shape[:2]
-    snaps = older + 1
+def gram(cells, now, start, around, axis):
+    samples, snaps, width = cells.shape
+    fields, _, rows, lanes = now.shape
     half = snaps // 2
     pair = 2
+    groups = samples // pair
     size = half + 8
     grouped = (fields, samples, ZSUB, rows, lanes)
+
+    def here(p):
+        return jnp.minimum(p, groups - 1)
 
     def below(which):
         return pl.BlockSpec(
             (fields, 1, rows, lanes),
-            lambda p: (0, jnp.maximum(ZSUB * (pair * p + which) - 1, 0), 0, 0),
+            lambda p: (0, jnp.maximum(ZSUB * (pair * here(p) + which) - 1, 0), 0, 0),
         )
 
     def plane(offset):
-        return pl.BlockSpec((fields, pair, 1, rows, lanes), lambda p: (0, p, offset, 0, 0))
-
-    whole = pl.BlockSpec((fields, rows, lanes), lambda p: (0, 0, 0))
-    line = pl.BlockSpec((fields, planes, lanes), lambda p: (0, 0, 0))
+        return pl.BlockSpec((fields, pair, 1, rows, lanes), lambda p: (0, here(p), offset, 0, 0))
+
+    in_vmem = pl.BlockSpec(memory_space=pltpu.VMEM)
     result = pl.BlockSpec((size, half), lambda p: (0, 0))
 
-    def body(older_ref, below_0, below_1, *refs):
-        gram_body(older_ref, (below_0, below_1), *refs, axis=axis)
+    def body(cells_ref, below_0, below_1, *refs):
+        gram_body(cells_ref, (below_0, below_1), *refs, axis=axis)
 
     return pl.pallas_call(
         body,
         out_shape=(jax.ShapeDtypeStruct((size, half), jnp.float32),) * 2,
-        grid=(samples // pair,),
+        grid=(groups + 1,),
         in_specs=[
-            pl.BlockSpec((older, pair, rows, lanes), lambda p: (0, p, 0, 0)),
-            below(0), below(1), plane(0), plane(1), plane(0), whole, whole, line, line,
+            pl.BlockSpec((pair, snaps, width), lambda p: (jnp.maximum(p - 1, 0), 0, 0)),
+            below(0), below(1), plane(0), plane(1), plane(0), in_vmem, in_vmem, in_vmem, in_vmem,
         ],
         out_specs=(result, result),
         scratch_shapes=[
-            pltpu.VMEM((snaps * rows, lanes), jnp.float32),
-            pltpu.VMEM((snaps * rows, lanes), jnp.float32),
+            pltpu.VMEM((pair, rows, lanes), jnp.float32),
             pltpu.VMEM((snaps, snaps), jnp.float32),
             pltpu.VMEM((fields, rows, lanes), jnp.float32),
             pltpu.VMEM((2 * size, half), jnp.float32),
         ],
         name="gram",
     )(
-        history, now, now, now.reshape(grouped), now.reshape(grouped), start.reshape(grouped), *around
+        cells, now, now, now.reshape(grouped), now.reshape(grouped), start.reshape(grouped), *around
     )
 
 
@@ -431,7 +464,8 @@
     x_a, x_b = neighbours(first, "gx", 1), neighbours(second, "gx", -1)
     y_a, y_b = neighbours(cols, "gy", 1), neighbours(cols, "gy", -1)
     around = (y_a, y_b, x_a, x_b)
-    mine, sent = gram(history, section_now, section_start, around, "gy")
+    cells = relayout(history)
+    mine, sent = gram(cells, section_now, section_start, around, "gy")
     mine = mine + swap(sent, 1)
     bit = 2
     while bit < count:

time: 68.1 us -> 75.3 us (1.11)
  Pallas kernels: 32.5 us -> 43.1 us
  starting transfers between devices: 15.3 us -> 9.09 us
  waiting for transfers between devices: 17 us -> 19.5 us
    pallas_call x0 -> x1, Pallas kernels: none -> 11 us  [relayout(): pl.pallas_call(relayout_body, out_shape=jax.ShapeDtypeStruct((samples, sn...]
    ppermute x6, starting transfers between devices: 7.12 us -> 0.95 us  [swap(): return lax.ppermute(part, axes, [(i, i ^ bit) for i in range(count)])]
    ppermute x6, waiting for transfers between devices: 13.6 us -> 19.4 us  [swap(): return lax.ppermute(part, axes, [(i, i ^ bit) for i in range(count)])]
    ppermute x4, waiting for transfers between devices: 3.41 us -> 0.01 us  [neighbours(): lax.ppermute(part, axis, [(i, (i + by * (-1) ** i) % size) for i in range...]
  transfers between devices with their start and end apart: 10 -> 10, of which waited for: 8 -> 5; matrix products, arithmetic and copies ran while one was open for 0% -> 0% of each run, Pallas kernels for 14% -> 28%
where the time goes in v1:
time: 75.3 us; the launch traced here: 74.6 us
  Pallas kernels  43.1 us (57%)
  waiting for transfers between devices  19.5 us (26%)
  starting transfers between devices  9.09 us (12%)
  local copies, waits for them, and re-layouts  1.31 us (2%)
  other arithmetic  0.93 us (1%)
    ppermute x6, waiting for transfers between devices, swap(): return lax.ppermute(part, axes, [(i, i ^ bit) for i in range(count)])  19.4 us
    pallas_call x1, Pallas kernels, relayout(): pl.pallas_call(relayout_body, out_shape=jax.ShapeDtypeStruct((samples, sn...  11 us
    pallas_call x1, Pallas kernels, gram(): pl.pallas_call(body, out_shape=(jax.ShapeDtypeStruct((size, half), jnp.fl...  9.89 us
    pallas_call x4, Pallas kernels, stencil(): pl.pallas_call(functools.partial(stencil_body, first), out_shape=jax.Shap...  9.74 us
    pallas_call x1, Pallas kernels, factor(): pl.pallas_call(functools.partial(factor_body, 1.0 / rows_total, axis), ou...  9.51 us
    ppermute x4, starting transfers between devices, neighbours(): lax.ppermute(part, axis, [(i, (i + by * (-1) ** i) % size) for i in range...  8.15 us
    pallas_call x1, Pallas kernels, edges(): pl.pallas_call(edges_body, out_shape=(line, line, jax.ShapeDtypeStruct((f...  2.92 us
  transfers between devices with their start and end apart: 10, of which 5 were waited for; matrix products, arithmetic and copies ran while one was open for 0% of the time, Pallas kernels for 28%

profile of v1, /device:TPU:0, one launch (start us, length us, event | category | flops | bytes accessed | tf_op | source)
XLA Modules:
  0.0 74.6 jit_solution(14080217209775524567)
XLA Ops:
  0.6 2.9 %edges.1 = (f32[5,64,128]{2,1,0:T(8,128)}, f32[5,64,128]{2,1,0:T(8,128)}, f32[5,8,128]{2,1,0:T(8,128)}) custom-call(f32[5,64,8,128]{3,2,1,0:T(8,128)} %below_1.1), custom_call_target="tpu_custom_call" | custom-call | tf_op jit(solution)/shard_map/edges/pallas_call | solution.py:51
  3.5 3.0 %collective-permute-start.2 = (f32[5,64,128]{2,1,0:T(8,128)}, f32[5,64,128]{2,1,0:T(8,128)S(1)}, u32[]{:S(2)}, u32[]{:S(2)}) collective-permute-start(f32[5,64,128]{2,1,0:T(8,128)} %get-tuple-element.8), channel_id=1, source_target_pairs={{0,4},{4,0},{8,12},{12,8},{16,20},{20,16},{24,28},{28,24},{1,5},{5... | collective-permute-start | bytes 491528 | tf_op jit(solution)/shard_map/ppermute | solution.py:459
  6.5 3.5 %collective-permute-start.3 = (f32[5,64,128]{2,1,0:T(8,128)}, f32[5,64,128]{2,1,0:T(8,128)S(1)}, u32[]{:S(2)}, u32[]{:S(2)}) collective-permute-start(f32[5,64,128]{2,1,0:T(8,128)} %get-tuple-element.9), channel_id=1, source_target_pairs={{0,28},{4,8},{8,4},{12,16},{16,12},{20,24},{24,20},{28,0},{1,29},{... | collective-permute-start | bytes 491528 | tf_op jit(solution)/shard_map/ppermute | solution.py:459
  10.1 1.6 %collective-permute-start.1 = (f32[5,8,128]{2,1,0:T(8,128)}, f32[5,8,128]{2,1,0:T(8,128)S(1)}, u32[]{:S(2)}, u32[]{:S(2)}) collective-permute-start(f32[5,8,128]{2,1,0:T(8,128)} %get-tuple-element.7), channel_id=1, source_target_pairs={{0,3},{1,2},{2,1},{3,0},{4,7},{5,6},{6,5},{7,4},{8,11},{9,10},{10,... | collective-permute-start | bytes 61448 | tf_op jit(solution)/shard_map/ppermute | solution.py:459
  11.7 11.0 %relayout.1.cells_ref = bf16[16,256,1024]{2,1,0:T(8,128)(2,1)} custom-call(bf16[255,16,8,128]{3,2,1,0:T(8,128)(2,1)} %older_ref.1), custom_call_target="tpu_custom_call" | custom-call | tf_op jit(solution)/shard_map/relayout/pallas_call | solution.py:235
  22.8 0.6 copy-done.2
  23.4 9.9 %gram.1 = (f32[136,128]{1,0:T(8,128)}, f32[136,128]{1,0:T(8,128)}) custom-call(bf16[16,256,1024]{2,1,0:T(8,128)(2,1)} %relayout.1.cells_ref, f32[5,64,8,128]{3,2,1,0:T(8,128)} %below_1.1, f32[5,64,8,128]{3,2,1,0:T(8,128)} %below_1.1, f32[5,16,4,8,128]{4,3,2,1,0:T(8,128)} %bitcast.2, f32[5,16,4,8,128]{4,3,2,1,0:T(8,128)} %bitcast.3, ...), custom_call_target="tpu_custom_call" | custom-call | tf_op jit(solution)/shard_map/gram/pallas_call | solution.py:341
  33.3 1.5 %collective-permute-done.4 = f32[136,128]{1,0:T(8,128)S(1)} collective-permute-done((f32[136,128]{1,0:T(8,128)}, f32[136,128]{1,0:T(8,128)S(1)}, u32[]{:S(2)}, u32[]{:S(2)}) %collective-permute-start.4) | collective-permute-done | bytes 69664 | tf_op jit(solution)/shard_map/ppermute | solution.py:462
  34.8 0.9 %add.15 = f32[136,128]{1,0:T(8,128)S(1)} add(f32[136,128]{1,0:T(8,128)} %get-tuple-element.10, f32[136,128]{1,0:T(8,128)S(1)} %collective-permute-done.4) | non-fusion elementwise | flops 17408 | bytes 208896 | tf_op jit(solution)/shard_map/add | solution.py:469
  35.7 0.6 collective-permute-start.5
  36.3 3.8 %collective-permute-done.5 = f32[136,128]{1,0:T(8,128)S(1)} collective-permute-done((f32[136,128]{1,0:T(8,128)S(1)}, f32[136,128]{1,0:T(8,128)S(1)}, u32[]{:S(2)}, u32[]{:S(2)}) %collective-permute-start.5) | collective-permute-done | bytes 69664 | tf_op jit(solution)/shard_map/ppermute | solution.py:462
  40.1 0.1 collective-permute-start.6
  40.2 4.3 %collective-permute-done.6 = f32[136,128]{1,0:T(8,128)S(1)} collective-permute-done((f32[136,128]{1,0:T(8,128)S(1)}, f32[136,128]{1,0:T(8,128)S(1)}, u32[]{:S(2)}, u32[]{:S(2)}) %collective-permute-start.6) | collective-permute-done | bytes 69664 | tf_op jit(solution)/shard_map/ppermute | solution.py:462
  44.5 0.1 collective-permute-start.7
  44.5 4.3 %collective-permute-done.7 = f32[136,128]{1,0:T(8,128)S(1)} collective-permute-done((f32[136,128]{1,0:T(8,128)S(1)}, f32[136,128]{1,0:T(8,128)S(1)}, u32[]{:S(2)}, u32[]{:S(2)}) %collective-permute-start.7) | collective-permute-done | bytes 69664 | tf_op jit(solution)/shard_map/ppermute | solution.py:462
  48.9 0.1 collective-permute-start.8
  49.0 5.6 %collective-permute-done.8 = f32[136,128]{1,0:T(8,128)S(1)} collective-permute-done((f32[136,128]{1,0:T(8,128)S(1)}, f32[136,128]{1,0:T(8,128)S(1)}, u32[]{:S(2)}, u32[]{:S(2)}) %collective-permute-start.8) | collective-permute-done | bytes 69664 | tf_op jit(solution)/shard_map/ppermute | solution.py:462
  54.6 0.1 collective-permute-start.9
  54.7 2.4 %shard_map.50.refs_8_ = f32[5,64,8,128]{3,2,1,0:T(8,128)} custom-call(f32[5,64,8,128]{3,2,1,0:T(8,128)} %below_1.1, f32[5,64,8,128]{3,2,1,0:T(8,128)} %below_1.1, f32[5,64,8,128]{3,2,1,0:T(8,128)} %below_1.1, f32[5,64,8,128]{3,2,1,0:T(8,128)} %refs_3_.7, f32[5,8,128]{2,1,0:T(8,128)} %copy-done.2, f32[5,8,128]{2,1,0:T(8,128)} %copy-done.3, ...), custom_call_target="tpu_custom_call" | custom-call | tf_op jit(solution)/shard_map/pallas_call | solution.py:201
  57.1 2.4 %shard_map.51.refs_8_ = f32[5,64,8,128]{3,2,1,0:T(8,128)} custom-call(f32[5,64,8,128]{3,2,1,0:T(8,128)} %below_1.1, f32[5,64,8,128]{3,2,1,0:T(8,128)} %below_1.1, f32[5,64,8,128]{3,2,1,0:T(8,128)} %below_1.1, f32[5,64,8,128]{3,2,1,0:T(8,128)} %refs_3_.7, f32[5,8,128]{2,1,0:T(8,128)} %copy-done.2, ...), custom_call_target="tpu_custom_call", output_to_operand_aliasing={{}: (8, {})} | custom-call | tf_op jit(solution)/shard_map/pallas_call | solution.py:201
  59.6 2.4 %shard_map.52.refs_8_ = f32[5,64,8,128]{3,2,1,0:T(8,128)} custom-call(f32[5,64,8,128]{3,2,1,0:T(8,128)} %below_1.1, f32[5,64,8,128]{3,2,1,0:T(8,128)} %below_1.1, f32[5,64,8,128]{3,2,1,0:T(8,128)} %below_1.1, f32[5,64,8,128]{3,2,1,0:T(8,128)} %refs_3_.7, f32[5,8,128]{2,1,0:T(8,128)} %copy-done.2, ...), custom_call_target="tpu_custom_call", output_to_operand_aliasing={{}: (8, {})} | custom-call | tf_op jit(solution)/shard_map/pallas_call | solution.py:201
  62.0 2.4 %shard_map.53 = f32[5,64,8,128]{3,2,1,0:T(8,128)} custom-call(f32[5,64,8,128]{3,2,1,0:T(8,128)} %below_1.1, f32[5,64,8,128]{3,2,1,0:T(8,128)} %below_1.1, f32[5,64,8,128]{3,2,1,0:T(8,128)} %below_1.1, f32[5,64,8,128]{3,2,1,0:T(8,128)} %refs_3_.7, f32[5,8,128]{2,1,0:T(8,128)} %copy-done.2, f32[5,8,128]{2,1,0:T(8,128)} %copy-done.3, ...), custom_call_target="tpu_custom_call", output_to_operand_aliasing={{}: (8, {})} | custom-call | tf_op jit(solution)/shard_map/pallas_call | solution.py:201
  64.5 0.6 copy-done.5
  65.1 9.5 %factor.1 = f32[256,256]{1,0:T(8,128)} custom-call(f32[136,128]{1,0:T(8,128)} %copy-done.4, f32[136,128]{1,0:T(8,128)} %copy-done.5), custom_call_target="tpu_custom_call" | custom-call | tf_op jit(solution)/shard_map/factor/pallas_call | solution.py:438
  (21 shorter events, 0.2 us)
Async XLA Ops:
  3.5 19.2 %collective-permute-start.2 = (f32[5,64,128]{2,1,0:T(8,128)}, f32[5,64,128]{2,1,0:T(8,128)S(1)}, u32[]{:S(2)}, u32[]{:S(2)}) collective-permute-start(f32[5,64,128]{2,1,0:T(8,128)} %get-tuple-element.8), channel_id=1, source_target_pairs={{0,4},{4,0},{8,12},{12,8},{16,20},{20,16},{24,28},{28,24},{1,5},{5... | collective-permute-start | bytes 491528 | tf_op jit(solution)/shard_map/ppermute | solution.py:459
  6.5 16.2 %collective-permute-start.3 = (f32[5,64,128]{2,1,0:T(8,128)}, f32[5,64,128]{2,1,0:T(8,128)S(1)}, u32[]{:S(2)}, u32[]{:S(2)}) collective-permute-start(f32[5,64,128]{2,1,0:T(8,128)} %get-tuple-element.9), channel_id=1, source_target_pairs={{0,28},{4,8},{8,4},{12,16},{16,12},{20,24},{24,20},{28,0},{1,29},{... | collective-permute-start | bytes 491528 | tf_op jit(solution)/shard_map/ppermute | solution.py:459
  10.1 12.6 %collective-permute-start = (f32[5,8,128]{2,1,0:T(8,128)}, f32[5,8,128]{2,1,0:T(8,128)S(1)}, u32[]{:S(2)}, u32[]{:S(2)}) collective-permute-start(f32[5,8,128]{2,1,0:T(8,128)} %get-tuple-element.7), channel_id=1, source_target_pairs={{0,1},{1,0},{2,3},{3,2},{4,5},{5,4},{6,7},{7,6},{8,9},{9,8},{10,11... | collective-permute-start | bytes 61448 | tf_op jit(solution)/shard_map/ppermute | solution.py:459
  10.1 12.6 %collective-permute-start.1 = (f32[5,8,128]{2,1,0:T(8,128)}, f32[5,8,128]{2,1,0:T(8,128)S(1)}, u32[]{:S(2)}, u32[]{:S(2)}) collective-permute-start(f32[5,8,128]{2,1,0:T(8,128)} %get-tuple-element.7), channel_id=1, source_target_pairs={{0,3},{1,2},{2,1},{3,0},{4,7},{5,6},{6,5},{7,4},{8,11},{9,10},{10,... | collective-permute-start | bytes 61448 | tf_op jit(solution)/shard_map/ppermute | solution.py:459
  22.7 0.6 copy-start.2
  22.7 0.6 copy-start.3
  22.7 0.7 copy-start
  22.7 0.7 copy-start.1
  33.3 1.5 %collective-permute-start.4 = (f32[136,128]{1,0:T(8,128)}, f32[136,128]{1,0:T(8,128)S(1)}, u32[]{:S(2)}, u32[]{:S(2)}) collective-permute-start(f32[136,128]{1,0:T(8,128)} %get-tuple-element.11), channel_id=1, source_target_pairs={{0,1},{1,0},{2,3},{3,2},{4,5},{5,4},{6,7},{7,6},{8,9},{9,8},{10,11... | collective-permute-start | bytes 208904 | tf_op jit(solution)/shard_map/ppermute | solution.py:462
  35.7 4.4 %collective-permute-start.5 = (f32[136,128]{1,0:T(8,128)S(1)}, f32[136,128]{1,0:T(8,128)S(1)}, u32[]{:S(2)}, u32[]{:S(2)}) collective-permute-start(f32[136,128]{1,0:T(8,128)S(1)} %add.15), channel_id=1, source_target_pairs={{0,2},{1,3},{2,0},{3,1},{4,6},{5,7},{6,4},{7,5},{8,10},{9,11},{10,... | collective-permute-start | bytes 208904 | tf_op jit(solution)/shard_map/ppermute | solution.py:462
  40.1 4.4 %collective-permute-start.6 = (f32[136,128]{1,0:T(8,128)S(1)}, f32[136,128]{1,0:T(8,128)S(1)}, u32[]{:S(2)}, u32[]{:S(2)}) collective-permute-start(f32[136,128]{1,0:T(8,128)S(1)} %add.16), channel_id=1, source_target_pairs={{0,4},{1,5},{2,6},{3,7},{4,0},{5,1},{6,2},{7,3},{8,12},{9,13},{10,... | collective-permute-start | bytes 208904 | tf_op jit(solution)/shard_map/ppermute | solution.py:462
  44.5 4.4 %collective-permute-start.7 = (f32[136,128]{1,0:T(8,128)S(1)}, f32[136,128]{1,0:T(8,128)S(1)}, u32[]{:S(2)}, u32[]{:S(2)}) collective-permute-start(f32[136,128]{1,0:T(8,128)S(1)} %add.17), channel_id=1, source_target_pairs={{0,8},{1,9},{2,10},{3,11},{4,12},{5,13},{6,14},{7,15},{8,0},{9,1},... | collective-permute-start | bytes 208904 | tf_op jit(solution)/shard_map/ppermute | solution.py:462
  48.9 5.7 %collective-permute-start.8 = (f32[136,128]{1,0:T(8,128)S(1)}, f32[136,128]{1,0:T(8,128)S(1)}, u32[]{:S(2)}, u32[]{:S(2)}) collective-permute-start(f32[136,128]{1,0:T(8,128)S(1)} %add.18), channel_id=1, source_target_pairs={{0,16},{1,17},{2,18},{3,19},{4,20},{5,21},{6,22},{7,23},{8,24},{9,... | collective-permute-start | bytes 208904 | tf_op jit(solution)/shard_map/ppermute | solution.py:462
  54.6 2.5 %copy-start.4 = (f32[136,128]{1,0:T(8,128)}, f32[136,128]{1,0:T(8,128)S(1)}, u32[]{:S(2)}) copy-start(f32[136,128]{1,0:T(8,128)S(1)} %add.19.mine_ref) | copy-start | bytes 208900
  54.6 9.8 %collective-permute-start.9 = (f32[136,128]{1,0:T(8,128)S(1)}, f32[136,128]{1,0:T(8,128)S(1)}, u32[]{:S(2)}, u32[]{:S(2)}) collective-permute-start(f32[136,128]{1,0:T(8,128)S(1)} %add.19.mine_ref), channel_id=1, source_target_pairs={{0,1},{1,0},{2,3},{3,2},{4,5},{5,4},{6,7},{7,6},{8,9},{9,8},{10,11... | collective-permute-start | bytes 208904 | tf_op jit(solution)/shard_map/ppermute | solution.py:462
  64.5 0.6 copy-start.5

commit v2 on v1

--- a/solution.py
+++ b/solution.py
@@ -14,6 +14,8 @@
 VISCOUS = 0.25
 CHUNK = 8
 PIECES = 4
+IN_VMEM = pl.BlockSpec(memory_space=pltpu.VMEM)
+ROOM = pltpu.CompilerParams(vmem_limit_bytes=20 * 1024 * 1024)
 
 
 def iota(shape, dim):
@@ -47,12 +49,12 @@
     fields, planes, rows, lanes = now.shape
     assert 2 * planes == lanes
     line = jax.ShapeDtypeStruct((fields, planes, lanes), now.dtype)
-    in_vmem = pl.BlockSpec(memory_space=pltpu.VMEM)
     return pl.pallas_call(
         edges_body,
         out_shape=(line, line, jax.ShapeDtypeStruct((fields, rows, lanes), now.dtype)),
-        in_specs=[in_vmem],
-        out_specs=(in_vmem, in_vmem, in_vmem),
+        in_specs=[IN_VMEM],
+        out_specs=(IN_VMEM, IN_VMEM, IN_VMEM),
+        compiler_params=ROOM,
         name="edges",
     )(now)
 
@@ -138,9 +140,10 @@
 
 
 def stencil_body(first, *refs):
-    now_ref, below_ref, above_ref, start_ref, y_a_ref, y_b_ref, x_a_ref, x_b_ref = refs[:8]
+    now_ref, start_ref, y_a_ref, y_b_ref, x_a_ref, x_b_ref = refs[:6]
     next_ref, halo_ref = refs[-2:]
-    fields, chunk, _, lanes = now_ref.shape
+    fields, chunk, _, lanes = next_ref.shape
+    planes = now_ref.shape[1]
     step = pl.program_id(0)
     base = (first + step) * chunk
     span = range(fields)
@@ -151,20 +154,23 @@
         for f in span:
             halo_ref[f] = packed[f]
 
-    x_lo, x_hi = sides("gx", [x_a_ref[f] for f in span], [x_b_ref[f] for f in span])
+    lines = pl.ds(pl.multiple_of(base, 8), chunk)
+    x_lo, x_hi = sides("gx", [x_a_ref[f, lines, :] for f in span], [x_b_ref[f, lines, :] for f in span])
     x_behind = only_behind(x_lo, 1)
     x_ahead = only_ahead(x_hi, 1)
     turn = lax.rem(lanes - 2 * base, lanes)
     halo = [pltpu.roll(halo_ref[f], turn, 1) for f in span]
-    before = only_behind([below_ref[f, 0] for f in span], 3)
+    z = jnp.maximum(base - 1, 0)
+    before = only_behind([now_ref[f, z] for f in span], 3)
     pending = None
 
     def finish(j, ahead):
         for f in span:
-            next_ref[f, j] = advanced(start_ref[f, j], now_ref[f, j], pending[f] + ahead[f])
+            total = pending[f] + ahead[f]
+            next_ref[f, j] = advanced(start_ref[f, base + j], now_ref[f, base + j], total)
 
     for j in range(chunk):
-        q = [now_ref[f, j] for f in span]
+        q = [now_ref[f, base + j] for f in span]
         state = state_of(q)
         products = products_of(q, state)
         half = scaled(q)
@@ -178,23 +184,15 @@
         )
         pending = [sums[f] + before[f] for f in span]
         before = behind_of(half, flux)
-    finish(chunk - 1, only_ahead([above_ref[f, 0] for f in span], 3))
+    z = jnp.minimum(base + chunk, planes - 1)
+    finish(chunk - 1, only_ahead([now_ref[f, z] for f in span], 3))
 
 
 def stencil(now, start, around, first, count, into):
-    fields, planes, rows, lanes = now.shape
+    fields, _, rows, lanes = now.shape
     chunk = CHUNK
-    whole = pl.BlockSpec((fields, rows, lanes), lambda c: (0, 0, 0))
-    part = pl.BlockSpec((fields, chunk, rows, lanes), lambda c: (0, first + c, 0, 0))
-    line = pl.BlockSpec((fields, chunk, lanes), lambda c: (0, first + c, 0))
-    below = pl.BlockSpec(
-        (fields, 1, rows, lanes), lambda c: (0, jnp.maximum((first + c) * chunk - 1, 0), 0, 0)
-    )
-    above = pl.BlockSpec(
-        (fields, 1, rows, lanes), lambda c: (0, jnp.minimum((first + c + 1) * chunk, planes - 1), 0, 0)
-    )
-    specs = [part, below, above, part, whole, whole, line, line]
-    operands = [now, now, now, start, *around]
+    specs = [IN_VMEM] * 6
+    operands = [now, start, *around]
     if into is not None:
         specs.append(pl.BlockSpec(memory_space=pl.ANY))
         operands.append(into)
@@ -203,15 +201,17 @@
         out_shape=jax.ShapeDtypeStruct(now.shape, now.dtype),
         grid=(count,),
         in_specs=specs,
-        out_specs=part,
+        out_specs=pl.BlockSpec((fields, chunk, rows, lanes), lambda c: (0, first + c, 0, 0)),
         scratch_shapes=[pltpu.VMEM((fields, rows, lanes), jnp.float32)],
         input_output_aliases={} if into is None else {len(operands) - 1: 0},
+        compiler_params=ROOM,
     )(*operands)
 
 
 def relayout_body(older_ref, out_ref, *cells_refs):
-    older, _, rows, lanes = older_ref.shape
+    older, pair, rows, lanes = older_ref.shape
     snaps = out_ref.shape[1]
+    base = pl.program_id(0) * pair
 
     @pl.when(pl.program_id(0) == 0)
     def _():
@@ -225,7 +225,7 @@
     for which, ref in enumerate(cells_refs):
         for r in range(rows):
             part = ref[pl.ds(r, snaps, stride=rows), :]
-            out_ref[which, :, r * lanes : (r + 1) * lanes] = part.astype(out_ref.dtype)
+            out_ref[base + which, :, r * lanes : (r + 1) * lanes] = part.astype(out_ref.dtype)
 
 
 def relayout(history):
@@ -237,19 +237,22 @@
         out_shape=jax.ShapeDtypeStruct((samples, snaps, rows * lanes), history.dtype),
         grid=(samples // pair,),
         in_specs=[pl.BlockSpec((older, pair, rows, lanes), lambda p: (0, p, 0, 0))],
-        out_specs=pl.BlockSpec((pair, snaps, rows * lanes), lambda p: (p, 0, 0)),
+        out_specs=IN_VMEM,
         scratch_shapes=[pltpu.VMEM((snaps * rows, lanes), jnp.float32)] * pair,
+        compiler_params=ROOM,
         name="relayout",
     )(history)
 
 
 def gram_body(
-    cells_ref, below_refs, now_ref, above_ref, start_ref, y_a_ref, y_b_ref, x_a_ref, x_b_ref,
+    cells_ref, now_ref, start_ref, y_a_ref, y_b_ref, x_a_ref, x_b_ref,
     mine_ref, sent_ref, newest_ref, total_ref, halo_ref, folded_ref, *, axis,
 ):
-    pair, snaps, width = cells_ref.shape
+    snaps, width = cells_ref.shape[1:]
+    pair = newest_ref.shape[0]
     fields, rows, lanes = halo_ref.shape
     step = pl.program_id(0)
+    base = pair * jnp.maximum(step - 1, 0)
     groups = pl.num_programs(0) - 1
     span = range(fields)
     tile = 16
@@ -265,9 +268,9 @@
     parts = []
     for which in range(pair):
         row = jnp.concatenate([newest_ref[which, r : r + 1, :] for r in range(rows)], axis=1)
-        last = cells_ref[which, snaps - tile :, :].astype(jnp.float32)
+        last = cells_ref[base + which, snaps - tile :, :].astype(jnp.float32)
         last = jnp.where(bottom, row, last).astype(cells_ref.dtype)
-        parts.append(jnp.concatenate([cells_ref[which, : snaps - tile, :], last], axis=0))
+        parts.append(jnp.concatenate([cells_ref[base + which, : snaps - tile, :], last], axis=0))
     matrix = jnp.concatenate(parts, axis=1)
     product = lax.dot_general(
         matrix, matrix, (((1,), (1,)), ((), ())), preferred_element_type=jnp.float32
@@ -275,7 +278,7 @@
 
     def newest(which):
         z = ZSUB * (pair * jnp.minimum(step, groups - 1) + which)
-        q = [now_ref[f, which, 0] for f in span]
+        q = [now_ref[f, z] for f in span]
         state = state_of(q)
         products = products_of(q, state)
         half = scaled(q)
@@ -286,9 +289,10 @@
         )
         x_behind, x_ahead = only_behind(x_lo, 1), only_ahead(x_hi, 1)
         sums = within_plane(q, half, state, products, edge, x_ahead, x_behind)
-        before = only_behind([below_refs[which][f, 0] for f in span], 3)
-        after = only_ahead([above_ref[f, which, 0] for f in span], 3)
-        out = [advanced(start_ref[f, which, 0], q[f], sums[f] + before[f] + after[f]) for f in span]
+        low = jnp.maximum(z - 1, 0)
+        before = only_behind([now_ref[f, low] for f in span], 3)
+        after = only_ahead([now_ref[f, z + 1] for f in span], 3)
+        out = [advanced(start_ref[f, z], q[f], sums[f] + before[f] + after[f]) for f in span]
         return state_of(out)[1]
 
     fresh = [newest(which) for which in range(pair)]
@@ -312,51 +316,27 @@
 
 
 def gram(cells, now, start, around, axis):
-    samples, snaps, width = cells.shape
+    samples, snaps, _ = cells.shape
     fields, _, rows, lanes = now.shape
     half = snaps // 2
     pair = 2
     groups = samples // pair
     size = half + 8
-    grouped = (fields, samples, ZSUB, rows, lanes)
-
-    def here(p):
-        return jnp.minimum(p, groups - 1)
-
-    def below(which):
-        return pl.BlockSpec(
-            (fields, 1, rows, lanes),
-            lambda p: (0, jnp.maximum(ZSUB * (pair * here(p) + which) - 1, 0), 0, 0),
-        )
-
-    def plane(offset):
-        return pl.BlockSpec((fields, pair, 1, rows, lanes), lambda p: (0, here(p), offset, 0, 0))
-
-    in_vmem = pl.BlockSpec(memory_space=pltpu.VMEM)
-    result = pl.BlockSpec((size, half), lambda p: (0, 0))
-
-    def body(cells_ref, below_0, below_1, *refs):
-        gram_body(cells_ref, (below_0, below_1), *refs, axis=axis)
-
     return pl.pallas_call(
-        body,
+        functools.partial(gram_body, axis=axis),
         out_shape=(jax.ShapeDtypeStruct((size, half), jnp.float32),) * 2,
         grid=(groups + 1,),
-        in_specs=[
-            pl.BlockSpec((pair, snaps, width), lambda p: (jnp.maximum(p - 1, 0), 0, 0)),
-            below(0), below(1), plane(0), plane(1), plane(0), in_vmem, in_vmem, in_vmem, in_vmem,
-        ],
-        out_specs=(result, result),
+        in_specs=[IN_VMEM] * 7,
+        out_specs=(IN_VMEM, IN_VMEM),
         scratch_shapes=[
             pltpu.VMEM((pair, rows, lanes), jnp.float32),
             pltpu.VMEM((snaps, snaps), jnp.float32),
             pltpu.VMEM((fields, rows, lanes), jnp.float32),
             pltpu.VMEM((2 * size, half), jnp.float32),
         ],
+        compiler_params=ROOM,
         name="gram",
-    )(
-        cells, now, now, now.reshape(grouped), now.reshape(grouped), start.reshape(grouped), *around
-    )
+    )(cells, now, start, *around)
 
 
 def factor_body(scale, axis, mine_ref, other_ref, out_ref, gram_ref, folded_ref):
@@ -434,16 +414,16 @@
 
 def factor(mine, other, rows_total, axis):
     size, half = mine.shape
-    in_vmem = pl.BlockSpec(memory_space=pltpu.VMEM)
     return pl.pallas_call(
         functools.partial(factor_body, 1.0 / rows_total, axis),
         out_shape=jax.ShapeDtypeStruct((2 * half, 2 * half), jnp.float32),
-        in_specs=[in_vmem, in_vmem],
-        out_specs=in_vmem,
+        in_specs=[IN_VMEM, IN_VMEM],
+        out_specs=IN_VMEM,
         scratch_shapes=[
             pltpu.VMEM((2 * half, 2 * half), jnp.float32),
             pltpu.VMEM((2 * size, half), jnp.float32),
         ],
+        compiler_params=ROOM,
         name="factor",
     )(mine, other)
 
@@ -464,7 +444,7 @@
     x_a, x_b = neighbours(first, "gx", 1), neighbours(second, "gx", -1)
     y_a, y_b = neighbours(cols, "gy", 1), neighbours(cols, "gy", -1)
     around = (y_a, y_b, x_a, x_b)
-    cells = relayout(history)
+    cells = relayout(pltpu.with_memory_space_constraint(history, pltpu.HBM))
     mine, sent = gram(cells, section_now, section_start, around, "gy")
     mine = mine + swap(sent, 1)
     bit = 2

time: 75.3 us -> 58.2 us (0.77)
  Pallas kernels: 43.1 us -> 27.3 us
  other arithmetic: 0.93 us -> 0.05 us
    pallas_call x1, Pallas kernels: 9.89 us -> 4.53 us  [gram(): pl.pallas_call(functools.partial(gram_body, axis=axis), out_shape=(jax.Sh...]
    pallas_call x4, Pallas kernels: 9.74 us -> 5.2 us  [stencil(): pl.pallas_call(functools.partial(stencil_body, first), out_shape=jax.Shap...]
    pallas_call x1, Pallas kernels: 11 us -> 8.07 us  [relayout(): pl.pallas_call(relayout_body, out_shape=jax.ShapeDtypeStruct((samples, sn...]
    pallas_call x1, Pallas kernels: 2.92 us -> 0.93 us  [edges(): pl.pallas_call(edges_body, out_shape=(line, line, jax.ShapeDtypeStruct((f...]
    pallas_call x1, Pallas kernels: 9.51 us -> 8.61 us  [factor(): pl.pallas_call(functools.partial(factor_body, 1.0 / rows_total, axis), ou...]
    add x1, other arithmetic: 0.89 us -> 0.01 us  [local(): mine = mine + swap(sent, 1)]
  transfers between devices with their start and end apart: 10 -> 10, of which waited for: 5 -> 5; matrix products, arithmetic and copies ran while one was open for 0% -> 0% of each run, Pallas kernels for 28% -> 23%
where the time goes in v2:
time: 58.2 us; the launch traced here: 57.9 us
  Pallas kernels  27.3 us (47%)
  waiting for transfers between devices  19.1 us (33%)
  starting transfers between devices  9.36 us (16%)
  local copies, waits for them, and re-layouts  1.32 us (2%)
  between operations  0.76 us (1%)
    ppermute x6, waiting for transfers between devices, swap(): return lax.ppermute(part, axes, [(i, i ^ bit) for i in range(count)])  19.1 us
    pallas_call x1, Pallas kernels, factor(): pl.pallas_call(functools.partial(factor_body, 1.0 / rows_total, axis), ou...  8.61 us
    ppermute x4, starting transfers between devices, neighbours(): lax.ppermute(part, axis, [(i, (i + by * (-1) ** i) % size) for i in range...  8.21 us
    pallas_call x1, Pallas kernels, relayout(): pl.pallas_call(relayout_body, out_shape=jax.ShapeDtypeStruct((samples, sn...  8.07 us
    pallas_call x4, Pallas kernels, stencil(): pl.pallas_call(functools.partial(stencil_body, first), out_shape=jax.Shap...  5.2 us
    pallas_call x1, Pallas kernels, gram(): pl.pallas_call(functools.partial(gram_body, axis=axis), out_shape=(jax.Sh...  4.53 us
    unnamed x6, local copies, waits for them, and re-layouts  1.32 us
  transfers between devices with their start and end apart: 10, of which 5 were waited for; matrix products, arithmetic and copies ran while one was open for 0% of the time, Pallas kernels for 23%

profile of v2, /device:TPU:0, one launch (start us, length us, event | category | flops | bytes accessed | tf_op | source)
XLA Modules:
  0.0 57.9 jit_solution(6014751897960298680)
XLA Ops:
  0.6 0.0 copy-start
  0.6 1.3 %copy-done = f32[5,64,8,128]{3,2,1,0:T(8,128)S(1)} copy-done((f32[5,64,8,128]{3,2,1,0:T(8,128)S(1)}, f32[5,64,8,128]{3,2,1,0:T(8,128)}, u32[]{:S(2)}) %copy-start) | copy-done | bytes 1310744
  1.9 0.9 %edges.1 = (f32[5,64,128]{2,1,0:T(8,128)S(1)}, f32[5,64,128]{2,1,0:T(8,128)S(1)}, f32[5,8,128]{2,1,0:T(8,128)S(1)}) custom-call(f32[5,64,8,128]{3,2,1,0:T(8,128)S(1)} %copy-done), custom_call_target="tpu_custom_call" | custom-call | tf_op jit(solution)/shard_map/edges/pallas_call | solution.py:52
  2.9 3.1 %collective-permute-start.2 = (f32[5,64,128]{2,1,0:T(8,128)S(1)}, f32[5,64,128]{2,1,0:T(8,128)S(1)}, u32[]{:S(2)}, u32[]{:S(2)}) collective-permute-start(f32[5,64,128]{2,1,0:T(8,128)S(1)} %get-tuple-element.8), channel_id=1, source_target_pairs={{0,4},{4,0},{8,12},{12,8},{16,20},{20,16},{24,28},{28,24},{1,5},{5... | collective-permute-start | bytes 491528 | tf_op jit(solution)/shard_map/ppermute | solution.py:439
  5.9 3.5 %collective-permute-start.3 = (f32[5,64,128]{2,1,0:T(8,128)S(1)}, f32[5,64,128]{2,1,0:T(8,128)S(1)}, u32[]{:S(2)}, u32[]{:S(2)}) collective-permute-start(f32[5,64,128]{2,1,0:T(8,128)S(1)} %get-tuple-element.9), channel_id=1, source_target_pairs={{0,28},{4,8},{8,4},{12,16},{16,12},{20,24},{24,20},{28,0},{1,29},{... | collective-permute-start | bytes 491528 | tf_op jit(solution)/shard_map/ppermute | solution.py:439
  9.5 1.6 %collective-permute-start.1 = (f32[5,8,128]{2,1,0:T(8,128)S(1)}, f32[5,8,128]{2,1,0:T(8,128)S(1)}, u32[]{:S(2)}, u32[]{:S(2)}) collective-permute-start(f32[5,8,128]{2,1,0:T(8,128)S(1)} %get-tuple-element.7), channel_id=1, source_target_pairs={{0,3},{1,2},{2,1},{3,0},{4,7},{5,6},{6,5},{7,4},{8,11},{9,10},{10,... | collective-permute-start | bytes 61448 | tf_op jit(solution)/shard_map/ppermute | solution.py:439
  11.1 8.1 %relayout.1.cells_ref = bf16[16,256,1024]{2,1,0:T(8,128)(2,1)S(1)} custom-call(bf16[255,16,8,128]{3,2,1,0:T(8,128)(2,1)} %older_ref.1), custom_call_target="tpu_custom_call" | custom-call | tf_op jit(solution)/shard_map/relayout/pallas_call | solution.py:235
  19.2 4.5 %gram.1 = (f32[136,128]{1,0:T(8,128)S(1)}, f32[136,128]{1,0:T(8,128)S(1)}) custom-call(bf16[16,256,1024]{2,1,0:T(8,128)(2,1)S(1)} %relayout.1.cells_ref, f32[5,64,8,128]{3,2,1,0:T(8,128)S(1)} %copy-done.1, f32[5,64,8,128]{3,2,1,0:T(8,128)S(1)} %copy-done.2, f32[5,8,128]{2,1,0:T(8,128)S(1)} %collective-permute-done.refs_2_.y_a_ref, ...), custom_call_target="tpu_custom_call" | custom-call | tf_op jit(solution)/shard_map/gram/pallas_call | solution.py:325
  23.8 0.1 collective-permute-start.4
  23.9 1.2 %collective-permute-done.4 = f32[136,128]{1,0:T(8,128)S(1)} collective-permute-done((f32[136,128]{1,0:T(8,128)S(1)}, f32[136,128]{1,0:T(8,128)S(1)}, u32[]{:S(2)}, u32[]{:S(2)}) %collective-permute-start.4) | collective-permute-done | bytes 69664 | tf_op jit(solution)/shard_map/ppermute | solution.py:442
  25.1 0.7 %collective-permute-start.5 = (f32[136,128]{1,0:T(8,128)S(1)}, f32[136,128]{1,0:T(8,128)S(1)}, u32[]{:S(2)}, u32[]{:S(2)}) collective-permute-start(f32[136,128]{1,0:T(8,128)S(1)} %add.15), channel_id=1, source_target_pairs={{0,2},{1,3},{2,0},{3,1},{4,6},{5,7},{6,4},{7,5},{8,10},{9,11},{10,... | collective-permute-start | bytes 208904 | tf_op jit(solution)/shard_map/ppermute | solution.py:442
  25.9 3.6 %collective-permute-done.5 = f32[136,128]{1,0:T(8,128)S(1)} collective-permute-done((f32[136,128]{1,0:T(8,128)S(1)}, f32[136,128]{1,0:T(8,128)S(1)}, u32[]{:S(2)}, u32[]{:S(2)}) %collective-permute-start.5) | collective-permute-done | bytes 69664 | tf_op jit(solution)/shard_map/ppermute | solution.py:442
  29.5 0.1 collective-permute-start.6
  29.6 4.3 %collective-permute-done.6 = f32[136,128]{1,0:T(8,128)S(1)} collective-permute-done((f32[136,128]{1,0:T(8,128)S(1)}, f32[136,128]{1,0:T(8,128)S(1)}, u32[]{:S(2)}, u32[]{:S(2)}) %collective-permute-start.6) | collective-permute-done | bytes 69664 | tf_op jit(solution)/shard_map/ppermute | solution.py:442
  33.9 0.1 collective-permute-start.7
  34.0 4.3 %collective-permute-done.7 = f32[136,128]{1,0:T(8,128)S(1)} collective-permute-done((f32[136,128]{1,0:T(8,128)S(1)}, f32[136,128]{1,0:T(8,128)S(1)}, u32[]{:S(2)}, u32[]{:S(2)}) %collective-permute-start.7) | collective-permute-done | bytes 69664 | tf_op jit(solution)/shard_map/ppermute | solution.py:442
  38.3 0.1 collective-permute-start.8
  38.4 5.6 %collective-permute-done.8 = f32[136,128]{1,0:T(8,128)S(1)} collective-permute-done((f32[136,128]{1,0:T(8,128)S(1)}, f32[136,128]{1,0:T(8,128)S(1)}, u32[]{:S(2)}, u32[]{:S(2)}) %collective-permute-start.8) | collective-permute-done | bytes 69664 | tf_op jit(solution)/shard_map/ppermute | solution.py:442
  44.0 0.1 collective-permute-start.9
  44.1 1.3 %shard_map.50.refs_6_ = f32[5,64,8,128]{3,2,1,0:T(8,128)} custom-call(f32[5,64,8,128]{3,2,1,0:T(8,128)S(1)} %copy-done.1, f32[5,64,8,128]{3,2,1,0:T(8,128)S(1)} %copy-done.2, f32[5,8,128]{2,1,0:T(8,128)S(1)} %collective-permute-done.refs_2_.y_a_ref, f32[5,8,128]{2,1,0:T(8,128)S(1)} %collective-permute-done.1.refs_3_.y_b_ref, ...), custom_call_target="tpu_custom_call" | custom-call | tf_op jit(solution)/shard_map/pallas_call | solution.py:199
  45.4 1.3 %shard_map.51.refs_6_ = f32[5,64,8,128]{3,2,1,0:T(8,128)} custom-call(f32[5,64,8,128]{3,2,1,0:T(8,128)S(1)} %copy-done.1, f32[5,64,8,128]{3,2,1,0:T(8,128)S(1)} %copy-done.2, f32[5,8,128]{2,1,0:T(8,128)S(1)} %collective-permute-done.refs_2_.y_a_ref, f32[5,8,128]{2,1,0:T(8,128)S(1)} %collective-permute-done.1.refs_3_.y_b_ref, ...), custom_call_target="tpu_custom_call", output_to_operand_aliasing={{}: (6, {})} | custom-call | tf_op jit(solution)/shard_map/pallas_call | solution.py:199
  46.7 1.3 %shard_map.52.refs_6_ = f32[5,64,8,128]{3,2,1,0:T(8,128)} custom-call(f32[5,64,8,128]{3,2,1,0:T(8,128)S(1)} %copy-done.1, f32[5,64,8,128]{3,2,1,0:T(8,128)S(1)} %copy-done.2, f32[5,8,128]{2,1,0:T(8,128)S(1)} %collective-permute-done.refs_2_.y_a_ref, f32[5,8,128]{2,1,0:T(8,128)S(1)} %collective-permute-done.1.refs_3_.y_b_ref, ...), custom_call_target="tpu_custom_call", output_to_operand_aliasing={{}: (6, {})} | custom-call | tf_op jit(solution)/shard_map/pallas_call | solution.py:199
  48.0 1.3 %shard_map.53 = f32[5,64,8,128]{3,2,1,0:T(8,128)} custom-call(f32[5,64,8,128]{3,2,1,0:T(8,128)S(1)} %copy-done.1, f32[5,64,8,128]{3,2,1,0:T(8,128)S(1)} %copy-done.2, f32[5,8,128]{2,1,0:T(8,128)S(1)} %collective-permute-done.refs_2_.y_a_ref, f32[5,8,128]{2,1,0:T(8,128)S(1)} %collective-permute-done.1.refs_3_.y_b_ref, ...), custom_call_target="tpu_custom_call", output_to_operand_aliasing={{}: (6, {})} | custom-call | tf_op jit(solution)/shard_map/pallas_call | solution.py:199
  49.3 8.6 %factor.1 = f32[256,256]{1,0:T(8,128)} custom-call(f32[136,128]{1,0:T(8,128)S(1)} %add.19.mine_ref, f32[136,128]{1,0:T(8,128)S(1)} %collective-permute-done.9.other_ref), custom_call_target="tpu_custom_call" | custom-call | tf_op jit(solution)/shard_map/factor/pallas_call | solution.py:417
  (15 shorter events, 0.1 us)
Async XLA Ops:
  0.6 1.3 %copy-start = (f32[5,64,8,128]{3,2,1,0:T(8,128)S(1)}, f32[5,64,8,128]{3,2,1,0:T(8,128)}, u32[]{:S(2)}) copy-start(f32[5,64,8,128]{3,2,1,0:T(8,128)} %now_ref.3) | copy-start | bytes 3932164
  2.9 16.3 %collective-permute-start.2 = (f32[5,64,128]{2,1,0:T(8,128)S(1)}, f32[5,64,128]{2,1,0:T(8,128)S(1)}, u32[]{:S(2)}, u32[]{:S(2)}) collective-permute-start(f32[5,64,128]{2,1,0:T(8,128)S(1)} %get-tuple-element.8), channel_id=1, source_target_pairs={{0,4},{4,0},{8,12},{12,8},{16,20},{20,16},{24,28},{28,24},{1,5},{5... | collective-permute-start | bytes 491528 | tf_op jit(solution)/shard_map/ppermute | solution.py:439
  5.9 13.3 %collective-permute-start.3 = (f32[5,64,128]{2,1,0:T(8,128)S(1)}, f32[5,64,128]{2,1,0:T(8,128)S(1)}, u32[]{:S(2)}, u32[]{:S(2)}) collective-permute-start(f32[5,64,128]{2,1,0:T(8,128)S(1)} %get-tuple-element.9), channel_id=1, source_target_pairs={{0,28},{4,8},{8,4},{12,16},{16,12},{20,24},{24,20},{28,0},{1,29},{... | collective-permute-start | bytes 491528 | tf_op jit(solution)/shard_map/ppermute | solution.py:439
  9.5 9.7 %copy-start.1 = (f32[5,64,8,128]{3,2,1,0:T(8,128)S(1)}, f32[5,64,8,128]{3,2,1,0:T(8,128)}, u32[]{:S(2)}) copy-start(f32[5,64,8,128]{3,2,1,0:T(8,128)} %now_ref.3) | copy-start | bytes 3932164
  9.5 9.7 %copy-start.2 = (f32[5,64,8,128]{3,2,1,0:T(8,128)S(1)}, f32[5,64,8,128]{3,2,1,0:T(8,128)}, u32[]{:S(2)}) copy-start(f32[5,64,8,128]{3,2,1,0:T(8,128)} %start_ref.1) | copy-start | bytes 3932164
  9.5 9.7 %collective-permute-start = (f32[5,8,128]{2,1,0:T(8,128)S(1)}, f32[5,8,128]{2,1,0:T(8,128)S(1)}, u32[]{:S(2)}, u32[]{:S(2)}) collective-permute-start(f32[5,8,128]{2,1,0:T(8,128)S(1)} %get-tuple-element.7), channel_id=1, source_target_pairs={{0,1},{1,0},{2,3},{3,2},{4,5},{5,4},{6,7},{7,6},{8,9},{9,8},{10,11... | collective-permute-start | bytes 61448 | tf_op jit(solution)/shard_map/ppermute | solution.py:439
  9.5 9.7 %collective-permute-start.1 = (f32[5,8,128]{2,1,0:T(8,128)S(1)}, f32[5,8,128]{2,1,0:T(8,128)S(1)}, u32[]{:S(2)}, u32[]{:S(2)}) collective-permute-start(f32[5,8,128]{2,1,0:T(8,128)S(1)} %get-tuple-element.7), channel_id=1, source_target_pairs={{0,3},{1,2},{2,1},{3,0},{4,7},{5,6},{6,5},{7,4},{8,11},{9,10},{10,... | collective-permute-start | bytes 61448 | tf_op jit(solution)/shard_map/ppermute | solution.py:439
  23.8 1.3 %collective-permute-start.4 = (f32[136,128]{1,0:T(8,128)S(1)}, f32[136,128]{1,0:T(8,128)S(1)}, u32[]{:S(2)}, u32[]{:S(2)}) collective-permute-start(f32[136,128]{1,0:T(8,128)S(1)} %get-tuple-element.11), channel_id=1, source_target_pairs={{0,1},{1,0},{2,3},{3,2},{4,5},{5,4},{6,7},{7,6},{8,9},{9,8},{10,11... | collective-permute-start | bytes 208904 | tf_op jit(solution)/shard_map/ppermute | solution.py:442
  25.1 4.4 %collective-permute-start.5 = (f32[136,128]{1,0:T(8,128)S(1)}, f32[136,128]{1,0:T(8,128)S(1)}, u32[]{:S(2)}, u32[]{:S(2)}) collective-permute-start(f32[136,128]{1,0:T(8,128)S(1)} %add.15), channel_id=1, source_target_pairs={{0,2},{1,3},{2,0},{3,1},{4,6},{5,7},{6,4},{7,5},{8,10},{9,11},{10,... | collective-permute-start | bytes 208904 | tf_op jit(solution)/shard_map/ppermute | solution.py:442
  29.5 4.4 %collective-permute-start.6 = (f32[136,128]{1,0:T(8,128)S(1)}, f32[136,128]{1,0:T(8,128)S(1)}, u32[]{:S(2)}, u32[]{:S(2)}) collective-permute-start(f32[136,128]{1,0:T(8,128)S(1)} %add.16), channel_id=1, source_target_pairs={{0,4},{1,5},{2,6},{3,7},{4,0},{5,1},{6,2},{7,3},{8,12},{9,13},{10,... | collective-permute-start | bytes 208904 | tf_op jit(solution)/shard_map/ppermute | solution.py:442
  33.9 4.4 %collective-permute-start.7 = (f32[136,128]{1,0:T(8,128)S(1)}, f32[136,128]{1,0:T(8,128)S(1)}, u32[]{:S(2)}, u32[]{:S(2)}) collective-permute-start(f32[136,128]{1,0:T(8,128)S(1)} %add.17), channel_id=1, source_target_pairs={{0,8},{1,9},{2,10},{3,11},{4,12},{5,13},{6,14},{7,15},{8,0},{9,1},... | collective-permute-start | bytes 208904 | tf_op jit(solution)/shard_map/ppermute | solution.py:442
  38.3 5.7 %collective-permute-start.8 = (f32[136,128]{1,0:T(8,128)S(1)}, f32[136,128]{1,0:T(8,128)S(1)}, u32[]{:S(2)}, u32[]{:S(2)}) collective-permute-start(f32[136,128]{1,0:T(8,128)S(1)} %add.18), channel_id=1, source_target_pairs={{0,16},{1,17},{2,18},{3,19},{4,20},{5,21},{6,22},{7,23},{8,24},{9,... | collective-permute-start | bytes 208904 | tf_op jit(solution)/shard_map/ppermute | solution.py:442
  44.0 5.3 %collective-permute-start.9 = (f32[136,128]{1,0:T(8,128)S(1)}, f32[136,128]{1,0:T(8,128)S(1)}, u32[]{:S(2)}, u32[]{:S(2)}) collective-permute-start(f32[136,128]{1,0:T(8,128)S(1)} %add.19.mine_ref), channel_id=1, source_target_pairs={{0,1},{1,0},{2,3},{3,2},{4,5},{5,4},{6,7},{7,6},{8,9},{9,8},{10,11... | collective-permute-start | bytes 208904 | tf_op jit(solution)/shard_map/ppermute | solution.py:442

commit v3 on v2

--- a/solution.py
+++ b/solution.py
@@ -209,36 +209,37 @@
 
 
 def relayout_body(older_ref, out_ref, *cells_refs):
-    older, pair, rows, lanes = older_ref.shape
+    older, group, rows, lanes = older_ref.shape
     snaps = out_ref.shape[1]
-    base = pl.program_id(0) * pair
+    base = pl.program_id(0) * group
+    stride = rows + 1
 
     @pl.when(pl.program_id(0) == 0)
     def _():
         for ref in cells_refs:
-            ref[pl.ds(older * rows, (snaps - older) * rows), :] = jnp.zeros(
-                ((snaps - older) * rows, lanes), jnp.float32
-            )
+            for snap in range(older, snaps):
+                ref[pl.ds(snap * stride, rows), :] = jnp.zeros((rows, lanes), jnp.float32)
 
     for which, ref in enumerate(cells_refs):
-        ref[pl.ds(0, older * rows), :] = older_ref[:, which].astype(jnp.float32).reshape(older * rows, lanes)
+        for snap in range(older):
+            ref[pl.ds(snap * stride, rows), :] = older_ref[snap, which].astype(jnp.float32)
     for which, ref in enumerate(cells_refs):
         for r in range(rows):
-            part = ref[pl.ds(r, snaps, stride=rows), :]
+            part = ref[pl.ds(r, snaps, stride=stride), :]
             out_ref[base + which, :, r * lanes : (r + 1) * lanes] = part.astype(out_ref.dtype)
 
 
 def relayout(history):
     older, samples, rows, lanes = history.shape
     snaps = older + 1
-    pair = 2
+    group = 4
     return pl.pallas_call(
         relayout_body,
         out_shape=jax.ShapeDtypeStruct((samples, snaps, rows * lanes), history.dtype),
-        grid=(samples // pair,),
-        in_specs=[pl.BlockSpec((older, pair, rows, lanes), lambda p: (0, p, 0, 0))],
+        grid=(samples // group,),
+        in_specs=[pl.BlockSpec((older, group, rows, lanes), lambda p: (0, p, 0, 0))],
         out_specs=IN_VMEM,
-        scratch_shapes=[pltpu.VMEM((snaps * rows, lanes), jnp.float32)] * pair,
+        scratch_shapes=[pltpu.VMEM((snaps * (rows + 1), lanes), jnp.float32)] * group,
         compiler_params=ROOM,
         name="relayout",
     )(history)
@@ -321,7 +322,7 @@
     half = snaps // 2
     pair = 2
     groups = samples // pair
-    size = half + 8
+    size = half + 16
     return pl.pallas_call(
         functools.partial(gram_body, axis=axis),
         out_shape=(jax.ShapeDtypeStruct((size, half), jnp.float32),) * 2,
@@ -446,13 +447,20 @@
     around = (y_a, y_b, x_a, x_b)
     cells = relayout(pltpu.with_memory_space_constraint(history, pltpu.HBM))
     mine, sent = gram(cells, section_now, section_start, around, "gy")
-    mine = mine + swap(sent, 1)
-    bit = 2
+    whole = mine + swap(sent, 1)
+    low = (lax.axis_index("gy") & 2) == 0
+    quarter = whole.shape[0] // 2
+    top, bottom = whole[:quarter], whole[quarter:]
+    part = jnp.where(low, top, bottom) + swap(jnp.where(low, bottom, top), 2)
+    bit = 4
     while bit < count:
-        mine = mine + swap(mine, bit)
+        part = part + swap(part, bit)
         bit *= 2
+    other = swap(part, 2)
+    whole = jnp.concatenate([jnp.where(low, part, other), jnp.where(low, other, part)])
     rows_total = history[0].size * count
-    triangle = factor(mine, swap(mine, 1), rows_total, "gy")
+    other = swap(whole, 1)
+    triangle = factor(whole, other, rows_total, "gy")
     chunks = section_now.shape[1] // CHUNK
     section_next = None
     for piece in range(PIECES):

time: 58.2 us -> 58.2 us (level)
  Pallas kernels: 27.3 us -> 25.2 us
  waiting for transfers between devices: 19.1 us -> 20.7 us
    pallas_call x1, Pallas kernels: 8.07 us -> 5.98 us  [relayout(): pl.pallas_call(relayout_body, out_shape=jax.ShapeDtypeStruct((samples, sn...]
    ppermute x6 -> x7, waiting for transfers between devices: 19.1 us -> 20.7 us  [swap(): return lax.ppermute(part, axes, [(i, i ^ bit) for i in range(count)])]
    ppermute x6 -> x7, starting transfers between devices: 1.15 us -> 1.67 us  [swap(): return lax.ppermute(part, axes, [(i, i ^ bit) for i in range(count)])]
  transfers between devices with their start and end apart: 10 -> 11, of which waited for: 5 -> 6; matrix products, arithmetic and copies ran while one was open for 0% -> 0% of each run, Pallas kernels for 23% -> 19%
where the time goes in v3:
time: 58.2 us; the launch traced here: 58 us
  Pallas kernels  25.2 us (43%)
  waiting for transfers between devices  20.7 us (36%)
  starting transfers between devices  9.88 us (17%)
  local copies, waits for them, and re-layouts  1.32 us (2%)
  between operations  0.78 us (1%)
    ppermute x7, waiting for transfers between devices, swap(): return lax.ppermute(part, axes, [(i, i ^ bit) for i in range(count)])  20.7 us
    pallas_call x1, Pallas kernels, factor(): pl.pallas_call(functools.partial(factor_body, 1.0 / rows_total, axis), ou...  8.6 us
    ppermute x4, starting transfers between devices, neighbours(): lax.ppermute(part, axis, [(i, (i + by * (-1) ** i) % size) for i in range...  8.21 us
    pallas_call x1, Pallas kernels, relayout(): pl.pallas_call(relayout_body, out_shape=jax.ShapeDtypeStruct((samples, sn...  5.98 us
    pallas_call x4, Pallas kernels, stencil(): pl.pallas_call(functools.partial(stencil_body, first), out_shape=jax.Shap...  5.2 us
    pallas_call x1, Pallas kernels, gram(): pl.pallas_call(functools.partial(gram_body, axis=axis), out_shape=(jax.Sh...  4.54 us
    ppermute x7, starting transfers between devices, swap(): return lax.ppermute(part, axes, [(i, i ^ bit) for i in range(count)])  1.67 us
    unnamed x6, local copies, waits for them, and re-layouts  1.32 us
  transfers between devices with their start and end apart: 11, of which 6 were waited for; matrix products, arithmetic and copies ran while one was open for 0% of the time, Pallas kernels for 19%

profile of v3, /device:TPU:0, one launch (start us, length us, event | category | flops | bytes accessed | tf_op | source)
XLA Modules:
  0.0 58.0 jit_solution(13473337374799619376)
XLA Ops:
  0.6 1.3 %copy-done = f32[5,64,8,128]{3,2,1,0:T(8,128)S(1)} copy-done((f32[5,64,8,128]{3,2,1,0:T(8,128)S(1)}, f32[5,64,8,128]{3,2,1,0:T(8,128)}, u32[]{:S(2)}) %copy-start) | copy-done | bytes 1310744
  1.9 0.9 %edges.1 = (f32[5,64,128]{2,1,0:T(8,128)S(1)}, f32[5,64,128]{2,1,0:T(8,128)S(1)}, f32[5,8,128]{2,1,0:T(8,128)S(1)}) custom-call(f32[5,64,8,128]{3,2,1,0:T(8,128)S(1)} %copy-done), custom_call_target="tpu_custom_call" | custom-call | tf_op jit(solution)/shard_map/edges/pallas_call | solution.py:52
  2.9 3.1 %collective-permute-start.2 = (f32[5,64,128]{2,1,0:T(8,128)S(1)}, f32[5,64,128]{2,1,0:T(8,128)S(1)}, u32[]{:S(2)}, u32[]{:S(2)}) collective-permute-start(f32[5,64,128]{2,1,0:T(8,128)S(1)} %get-tuple-element.8), channel_id=1, source_target_pairs={{0,4},{4,0},{8,12},{12,8},{16,20},{20,16},{24,28},{28,24},{1,5},{5... | collective-permute-start | bytes 491528 | tf_op jit(solution)/shard_map/ppermute | solution.py:440
  5.9 3.5 %collective-permute-start.3 = (f32[5,64,128]{2,1,0:T(8,128)S(1)}, f32[5,64,128]{2,1,0:T(8,128)S(1)}, u32[]{:S(2)}, u32[]{:S(2)}) collective-permute-start(f32[5,64,128]{2,1,0:T(8,128)S(1)} %get-tuple-element.9), channel_id=1, source_target_pairs={{0,28},{4,8},{8,4},{12,16},{16,12},{20,24},{24,20},{28,0},{1,29},{... | collective-permute-start | bytes 491528 | tf_op jit(solution)/shard_map/ppermute | solution.py:440
  9.5 1.6 %collective-permute-start.1 = (f32[5,8,128]{2,1,0:T(8,128)S(1)}, f32[5,8,128]{2,1,0:T(8,128)S(1)}, u32[]{:S(2)}, u32[]{:S(2)}) collective-permute-start(f32[5,8,128]{2,1,0:T(8,128)S(1)} %get-tuple-element.7), channel_id=1, source_target_pairs={{0,3},{1,2},{2,1},{3,0},{4,7},{5,6},{6,5},{7,4},{8,11},{9,10},{10,... | collective-permute-start | bytes 61448 | tf_op jit(solution)/shard_map/ppermute | solution.py:440
  11.1 6.0 %relayout.1.cells_ref = bf16[16,256,1024]{2,1,0:T(8,128)(2,1)S(1)} custom-call(bf16[255,16,8,128]{3,2,1,0:T(8,128)(2,1)} %older_ref.1), custom_call_target="tpu_custom_call" | custom-call | tf_op jit(solution)/shard_map/relayout/pallas_call | solution.py:236
  17.1 4.5 %gram.1 = (f32[144,128]{1,0:T(8,128)S(1)}, f32[144,128]{1,0:T(8,128)S(1)}) custom-call(bf16[16,256,1024]{2,1,0:T(8,128)(2,1)S(1)} %relayout.1.cells_ref, f32[5,64,8,128]{3,2,1,0:T(8,128)S(1)} %copy-done.1, f32[5,64,8,128]{3,2,1,0:T(8,128)S(1)} %copy-done.2, f32[5,8,128]{2,1,0:T(8,128)S(1)} %collective-permute-done.refs_2_.y_a_ref, ...), custom_call_target="tpu_custom_call" | custom-call | tf_op jit(solution)/shard_map/gram/pallas_call | solution.py:326
  21.7 0.1 collective-permute-start.4
  21.8 1.2 %collective-permute-done.4 = f32[144,128]{1,0:T(8,128)S(1)} collective-permute-done((f32[144,128]{1,0:T(8,128)S(1)}, f32[144,128]{1,0:T(8,128)S(1)}, u32[]{:S(2)}, u32[]{:S(2)}) %collective-permute-start.4) | collective-permute-done | bytes 73760 | tf_op jit(solution)/shard_map/ppermute | solution.py:443
  23.1 0.7 %collective-permute-start.5 = (f32[72,128]{1,0:T(8,128)S(1)}, f32[72,128]{1,0:T(8,128)S(1)}, u32[]{:S(2)}, u32[]{:S(2)}) collective-permute-start(f32[72,128]{1,0:T(8,128)S(1)} %slice_select_fusion), channel_id=1, source_target_pairs={{0,2},{1,3},{2,0},{3,1},{4,6},{5,7},{6,4},{7,5},{8,10},{9,11},{10,... | collective-permute-start | bytes 110600 | tf_op jit(solution)/shard_map/ppermute | solution.py:443
  23.8 3.3 %collective-permute-done.5 = f32[72,128]{1,0:T(8,128)S(1)} collective-permute-done((f32[72,128]{1,0:T(8,128)S(1)}, f32[72,128]{1,0:T(8,128)S(1)}, u32[]{:S(2)}, u32[]{:S(2)}) %collective-permute-start.5) | collective-permute-done | bytes 36896 | tf_op jit(solution)/shard_map/ppermute | solution.py:443
  27.1 0.1 collective-permute-start.6
  27.2 3.9 %collective-permute-done.6 = f32[72,128]{1,0:T(8,128)S(1)} collective-permute-done((f32[72,128]{1,0:T(8,128)S(1)}, f32[72,128]{1,0:T(8,128)S(1)}, u32[]{:S(2)}, u32[]{:S(2)}) %collective-permute-start.6) | collective-permute-done | bytes 36896 | tf_op jit(solution)/shard_map/ppermute | solution.py:443
  31.1 3.9 %collective-permute-done.7 = f32[72,128]{1,0:T(8,128)S(1)} collective-permute-done((f32[72,128]{1,0:T(8,128)S(1)}, f32[72,128]{1,0:T(8,128)S(1)}, u32[]{:S(2)}, u32[]{:S(2)}) %collective-permute-start.7) | collective-permute-done | bytes 36896 | tf_op jit(solution)/shard_map/ppermute | solution.py:443
  35.1 0.1 collective-permute-start.8
  35.2 5.0 %collective-permute-done.8 = f32[72,128]{1,0:T(8,128)S(1)} collective-permute-done((f32[72,128]{1,0:T(8,128)S(1)}, f32[72,128]{1,0:T(8,128)S(1)}, u32[]{:S(2)}, u32[]{:S(2)}) %collective-permute-start.8) | collective-permute-done | bytes 36896 | tf_op jit(solution)/shard_map/ppermute | solution.py:443
  40.1 0.7 %collective-permute-start.9 = (f32[72,128]{1,0:T(8,128)S(1)}, f32[72,128]{1,0:T(8,128)S(1)}, u32[]{:S(2)}, u32[]{:S(2)}) collective-permute-start(f32[72,128]{1,0:T(8,128)S(1)} %add.19), channel_id=1, source_target_pairs={{0,2},{1,3},{2,0},{3,1},{4,6},{5,7},{6,4},{7,5},{8,10},{9,11},{10,... | collective-permute-start | bytes 110600 | tf_op jit(solution)/shard_map/ppermute | solution.py:443
  40.8 3.3 %collective-permute-done.9 = f32[72,128]{1,0:T(8,128)S(1)} collective-permute-done((f32[72,128]{1,0:T(8,128)S(1)}, f32[72,128]{1,0:T(8,128)S(1)}, u32[]{:S(2)}, u32[]{:S(2)}) %collective-permute-start.9) | collective-permute-done | bytes 36896 | tf_op jit(solution)/shard_map/ppermute | solution.py:443
  44.1 0.1 collective-permute-start.10
  44.2 1.3 %shard_map.50.refs_6_ = f32[5,64,8,128]{3,2,1,0:T(8,128)} custom-call(f32[5,64,8,128]{3,2,1,0:T(8,128)S(1)} %copy-done.1, f32[5,64,8,128]{3,2,1,0:T(8,128)S(1)} %copy-done.2, f32[5,8,128]{2,1,0:T(8,128)S(1)} %collective-permute-done.refs_2_.y_a_ref, f32[5,8,128]{2,1,0:T(8,128)S(1)} %collective-permute-done.1.refs_3_.y_b_ref, ...), custom_call_target="tpu_custom_call" | custom-call | tf_op jit(solution)/shard_map/pallas_call | solution.py:199
  45.5 1.3 %shard_map.51.refs_6_ = f32[5,64,8,128]{3,2,1,0:T(8,128)} custom-call(f32[5,64,8,128]{3,2,1,0:T(8,128)S(1)} %copy-done.1, f32[5,64,8,128]{3,2,1,0:T(8,128)S(1)} %copy-done.2, f32[5,8,128]{2,1,0:T(8,128)S(1)} %collective-permute-done.refs_2_.y_a_ref, f32[5,8,128]{2,1,0:T(8,128)S(1)} %collective-permute-done.1.refs_3_.y_b_ref, ...), custom_call_target="tpu_custom_call", output_to_operand_aliasing={{}: (6, {})} | custom-call | tf_op jit(solution)/shard_map/pallas_call | solution.py:199
  46.8 1.3 %shard_map.52.refs_6_ = f32[5,64,8,128]{3,2,1,0:T(8,128)} custom-call(f32[5,64,8,128]{3,2,1,0:T(8,128)S(1)} %copy-done.1, f32[5,64,8,128]{3,2,1,0:T(8,128)S(1)} %copy-done.2, f32[5,8,128]{2,1,0:T(8,128)S(1)} %collective-permute-done.refs_2_.y_a_ref, f32[5,8,128]{2,1,0:T(8,128)S(1)} %collective-permute-done.1.refs_3_.y_b_ref, ...), custom_call_target="tpu_custom_call", output_to_operand_aliasing={{}: (6, {})} | custom-call | tf_op jit(solution)/shard_map/pallas_call | solution.py:199
  48.1 1.3 %shard_map.53 = f32[5,64,8,128]{3,2,1,0:T(8,128)} custom-call(f32[5,64,8,128]{3,2,1,0:T(8,128)S(1)} %copy-done.1, f32[5,64,8,128]{3,2,1,0:T(8,128)S(1)} %copy-done.2, f32[5,8,128]{2,1,0:T(8,128)S(1)} %collective-permute-done.refs_2_.y_a_ref, f32[5,8,128]{2,1,0:T(8,128)S(1)} %collective-permute-done.1.refs_3_.y_b_ref, ...), custom_call_target="tpu_custom_call", output_to_operand_aliasing={{}: (6, {})} | custom-call | tf_op jit(solution)/shard_map/pallas_call | solution.py:199
  49.4 8.6 %factor.1 = f32[256,256]{1,0:T(8,128)} custom-call(f32[144,128]{1,0:T(8,128)S(1)} %pad_maximum_fusion.mine_ref, f32[144,128]{1,0:T(8,128)S(1)} %collective-permute-done.10.other_ref), custom_call_target="tpu_custom_call" | custom-call | tf_op jit(solution)/shard_map/factor/pallas_call | solution.py:418
  (20 shorter events, 0.1 us)
Async XLA Ops:
  0.6 1.3 %copy-start = (f32[5,64,8,128]{3,2,1,0:T(8,128)S(1)}, f32[5,64,8,128]{3,2,1,0:T(8,128)}, u32[]{:S(2)}) copy-start(f32[5,64,8,128]{3,2,1,0:T(8,128)} %now_ref.3) | copy-start | bytes 3932164
  2.9 14.2 %collective-permute-start.2 = (f32[5,64,128]{2,1,0:T(8,128)S(1)}, f32[5,64,128]{2,1,0:T(8,128)S(1)}, u32[]{:S(2)}, u32[]{:S(2)}) collective-permute-start(f32[5,64,128]{2,1,0:T(8,128)S(1)} %get-tuple-element.8), channel_id=1, source_target_pairs={{0,4},{4,0},{8,12},{12,8},{16,20},{20,16},{24,28},{28,24},{1,5},{5... | collective-permute-start | bytes 491528 | tf_op jit(solution)/shard_map/ppermute | solution.py:440
  5.9 11.2 %collective-permute-start.3 = (f32[5,64,128]{2,1,0:T(8,128)S(1)}, f32[5,64,128]{2,1,0:T(8,128)S(1)}, u32[]{:S(2)}, u32[]{:S(2)}) collective-permute-start(f32[5,64,128]{2,1,0:T(8,128)S(1)} %get-tuple-element.9), channel_id=1, source_target_pairs={{0,28},{4,8},{8,4},{12,16},{16,12},{20,24},{24,20},{28,0},{1,29},{... | collective-permute-start | bytes 491528 | tf_op jit(solution)/shard_map/ppermute | solution.py:440
  9.5 7.6 %copy-start.1 = (f32[5,64,8,128]{3,2,1,0:T(8,128)S(1)}, f32[5,64,8,128]{3,2,1,0:T(8,128)}, u32[]{:S(2)}) copy-start(f32[5,64,8,128]{3,2,1,0:T(8,128)} %now_ref.3) | copy-start | bytes 3932164
  9.5 7.6 %copy-start.2 = (f32[5,64,8,128]{3,2,1,0:T(8,128)S(1)}, f32[5,64,8,128]{3,2,1,0:T(8,128)}, u32[]{:S(2)}) copy-start(f32[5,64,8,128]{3,2,1,0:T(8,128)} %start_ref.1) | copy-start | bytes 3932164
  9.5 7.6 %collective-permute-start = (f32[5,8,128]{2,1,0:T(8,128)S(1)}, f32[5,8,128]{2,1,0:T(8,128)S(1)}, u32[]{:S(2)}, u32[]{:S(2)}) collective-permute-start(f32[5,8,128]{2,1,0:T(8,128)S(1)} %get-tuple-element.7), channel_id=1, source_target_pairs={{0,1},{1,0},{2,3},{3,2},{4,5},{5,4},{6,7},{7,6},{8,9},{9,8},{10,11... | collective-permute-start | bytes 61448 | tf_op jit(solution)/shard_map/ppermute | solution.py:440
  9.5 7.6 %collective-permute-start.1 = (f32[5,8,128]{2,1,0:T(8,128)S(1)}, f32[5,8,128]{2,1,0:T(8,128)S(1)}, u32[]{:S(2)}, u32[]{:S(2)}) collective-permute-start(f32[5,8,128]{2,1,0:T(8,128)S(1)} %get-tuple-element.7), channel_id=1, source_target_pairs={{0,3},{1,2},{2,1},{3,0},{4,7},{5,6},{6,5},{7,4},{8,11},{9,10},{10,... | collective-permute-start | bytes 61448 | tf_op jit(solution)/shard_map/ppermute | solution.py:440
  21.7 1.3 %collective-permute-start.4 = (f32[144,128]{1,0:T(8,128)S(1)}, f32[144,128]{1,0:T(8,128)S(1)}, u32[]{:S(2)}, u32[]{:S(2)}) collective-permute-start(f32[144,128]{1,0:T(8,128)S(1)} %get-tuple-element.11), channel_id=1, source_target_pairs={{0,1},{1,0},{2,3},{3,2},{4,5},{5,4},{6,7},{7,6},{8,9},{9,8},{10,11... | collective-permute-start | bytes 221192 | tf_op jit(solution)/shard_map/ppermute | solution.py:443
  23.1 4.0 %collective-permute-start.5 = (f32[72,128]{1,0:T(8,128)S(1)}, f32[72,128]{1,0:T(8,128)S(1)}, u32[]{:S(2)}, u32[]{:S(2)}) collective-permute-start(f32[72,128]{1,0:T(8,128)S(1)} %slice_select_fusion), channel_id=1, source_target_pairs={{0,2},{1,3},{2,0},{3,1},{4,6},{5,7},{6,4},{7,5},{8,10},{9,11},{10,... | collective-permute-start | bytes 110600 | tf_op jit(solution)/shard_map/ppermute | solution.py:443
  27.1 4.0 %collective-permute-start.6 = (f32[72,128]{1,0:T(8,128)S(1)}, f32[72,128]{1,0:T(8,128)S(1)}, u32[]{:S(2)}, u32[]{:S(2)}) collective-permute-start(f32[72,128]{1,0:T(8,128)S(1)} %select_add_fusion), channel_id=1, source_target_pairs={{0,4},{1,5},{2,6},{3,7},{4,0},{5,1},{6,2},{7,3},{8,12},{9,13},{10,... | collective-permute-start | bytes 110600 | tf_op jit(solution)/shard_map/ppermute | solution.py:443
  31.1 4.0 %collective-permute-start.7 = (f32[72,128]{1,0:T(8,128)S(1)}, f32[72,128]{1,0:T(8,128)S(1)}, u32[]{:S(2)}, u32[]{:S(2)}) collective-permute-start(f32[72,128]{1,0:T(8,128)S(1)} %add.17), channel_id=1, source_target_pairs={{0,8},{1,9},{2,10},{3,11},{4,12},{5,13},{6,14},{7,15},{8,0},{9,1},... | collective-permute-start | bytes 110600 | tf_op jit(solution)/shard_map/ppermute | solution.py:443
  35.1 5.0 %collective-permute-start.8 = (f32[72,128]{1,0:T(8,128)S(1)}, f32[72,128]{1,0:T(8,128)S(1)}, u32[]{:S(2)}, u32[]{:S(2)}) collective-permute-start(f32[72,128]{1,0:T(8,128)S(1)} %add.18), channel_id=1, source_target_pairs={{0,16},{1,17},{2,18},{3,19},{4,20},{5,21},{6,22},{7,23},{8,24},{9,... | collective-permute-start | bytes 110600 | tf_op jit(solution)/shard_map/ppermute | solution.py:443
  40.1 4.0 %collective-permute-start.9 = (f32[72,128]{1,0:T(8,128)S(1)}, f32[72,128]{1,0:T(8,128)S(1)}, u32[]{:S(2)}, u32[]{:S(2)}) collective-permute-start(f32[72,128]{1,0:T(8,128)S(1)} %add.19), channel_id=1, source_target_pairs={{0,2},{1,3},{2,0},{3,1},{4,6},{5,7},{6,4},{7,5},{8,10},{9,11},{10,... | collective-permute-start | bytes 110600 | tf_op jit(solution)/shard_map/ppermute | solution.py:443
  44.1 5.3 %collective-permute-start.10 = (f32[144,128]{1,0:T(8,128)S(1)}, f32[144,128]{1,0:T(8,128)S(1)}, u32[]{:S(2)}, u32[]{:S(2)}) collective-permute-start(f32[144,128]{1,0:T(8,128)S(1)} %pad_maximum_fusion.mine_ref), channel_id=1, source_target_pairs={{0,1},{1,0},{2,3},{3,2},{4,5},{5,4},{6,7},{7,6},{8,9},{9,8},{10,11... | collective-permute-start | bytes 221192 | tf_op jit(solution)/shard_map/ppermute | solution.py:443

commit v4 on v3

--- a/solution.py
+++ b/solution.py
@@ -16,6 +16,7 @@
 PIECES = 4
 IN_VMEM = pl.BlockSpec(memory_space=pltpu.VMEM)
 ROOM = pltpu.CompilerParams(vmem_limit_bytes=20 * 1024 * 1024)
+SPREAD = pltpu.CompilerParams(vmem_limit_bytes=20 * 1024 * 1024)
 
 
 def iota(shape, dim):
@@ -322,7 +323,7 @@
     half = snaps // 2
     pair = 2
     groups = samples // pair
-    size = half + 16
+    size = half + 8
     return pl.pallas_call(
         functools.partial(gram_body, axis=axis),
         out_shape=(jax.ShapeDtypeStruct((size, half), jnp.float32),) * 2,
@@ -335,7 +336,7 @@
             pltpu.VMEM((fields, rows, lanes), jnp.float32),
             pltpu.VMEM((2 * size, half), jnp.float32),
         ],
-        compiler_params=ROOM,
+        compiler_params=SPREAD,
         name="gram",
     )(cells, now, start, *around)
 
@@ -429,6 +430,15 @@
     )(mine, other)
 
 
+def rounds(count):
+    groups = []
+    bit = 2
+    while bit < count:
+        groups.append((bit, 2 * bit, 3 * bit) if 2 * bit < count else (bit,))
+        bit *= 4
+    return groups
+
+
 def local(section_start, section_now, history):
     axes = ("gx", "gy")
     count = lax.axis_size("gx") * lax.axis_size("gy")
@@ -447,20 +457,14 @@
     around = (y_a, y_b, x_a, x_b)
     cells = relayout(pltpu.with_memory_space_constraint(history, pltpu.HBM))
     mine, sent = gram(cells, section_now, section_start, around, "gy")
-    whole = mine + swap(sent, 1)
-    low = (lax.axis_index("gy") & 2) == 0
-    quarter = whole.shape[0] // 2
-    top, bottom = whole[:quarter], whole[quarter:]
-    part = jnp.where(low, top, bottom) + swap(jnp.where(low, bottom, top), 2)
-    bit = 4
-    while bit < count:
-        part = part + swap(part, bit)
-        bit *= 2
-    other = swap(part, 2)
-    whole = jnp.concatenate([jnp.where(low, part, other), jnp.where(low, other, part)])
+    part = mine + swap(sent, 1)
+    for group in rounds(count):
+        came = [swap(part, bits) for bits in group]
+        part = part + came[0]
+        if len(came) > 1:
+            part = part + (came[1] + came[2])
     rows_total = history[0].size * count
-    other = swap(whole, 1)
-    triangle = factor(whole, other, rows_total, "gy")
+    triangle = factor(part, swap(part, 1), rows_total, "gy")
     chunks = section_now.shape[1] // CHUNK
     section_next = None
     for piece in range(PIECES):

time: 58.2 us -> 51.4 us (0.88)
  waiting for transfers between devices: 20.7 us -> 7.51 us
  starting transfers between devices: 9.88 us -> 16.4 us
    ppermute x7 -> x8, waiting for transfers between devices: 20.7 us -> 7.5 us  [swap(): return lax.ppermute(part, axes, [(i, i ^ bit) for i in range(count)])]
    ppermute x7 -> x8, starting transfers between devices: 1.67 us -> 8.15 us  [swap(): return lax.ppermute(part, axes, [(i, i ^ bit) for i in range(count)])]
  transfers between devices with their start and end apart: 11 -> 12, of which waited for: 6 -> 5; matrix products, arithmetic and copies ran while one was open for 0% -> 0% of each run, Pallas kernels for 19% -> 22%
where the time goes in v4:
time: 51.4 us; the launch traced here: 51.2 us
  Pallas kernels  25.3 us (49%)
  starting transfers between devices  16.4 us (32%)
  waiting for transfers between devices  7.51 us (15%)
  local copies, waits for them, and re-layouts  1.32 us (3%)
  between operations  0.74 us (1%)
    pallas_call x1, Pallas kernels, factor(): pl.pallas_call(functools.partial(factor_body, 1.0 / rows_total, axis), ou...  8.61 us
    ppermute x4, starting transfers between devices, neighbours(): lax.ppermute(part, axis, [(i, (i + by * (-1) ** i) % size) for i in range...  8.21 us
    ppermute x8, starting transfers between devices, swap(): return lax.ppermute(part, axes, [(i, i ^ bit) for i in range(count)])  8.15 us
    ppermute x8, waiting for transfers between devices, swap(): return lax.ppermute(part, axes, [(i, i ^ bit) for i in range(count)])  7.5 us
    pallas_call x1, Pallas kernels, relayout(): pl.pallas_call(relayout_body, out_shape=jax.ShapeDtypeStruct((samples, sn...  5.98 us
    pallas_call x4, Pallas kernels, stencil(): pl.pallas_call(functools.partial(stencil_body, first), out_shape=jax.Shap...  5.2 us
    pallas_call x1, Pallas kernels, gram(): pl.pallas_call(functools.partial(gram_body, axis=axis), out_shape=(jax.Sh...  4.54 us
    unnamed x6, local copies, waits for them, and re-layouts  1.32 us
  transfers between devices with their start and end apart: 12, of which 5 were waited for; matrix products, arithmetic and copies ran while one was open for 0% of the time, Pallas kernels for 22%

profile of v4, /device:TPU:0, one launch (start us, length us, event | category | flops | bytes accessed | tf_op | source)
XLA Modules:
  0.0 51.2 jit_solution(13487847157511340247)
XLA Ops:
  0.6 0.0 copy-start
  0.6 1.3 %copy-done = f32[5,64,8,128]{3,2,1,0:T(8,128)S(1)} copy-done((f32[5,64,8,128]{3,2,1,0:T(8,128)S(1)}, f32[5,64,8,128]{3,2,1,0:T(8,128)}, u32[]{:S(2)}) %copy-start) | copy-done | bytes 1310744
  1.9 0.9 %edges.1 = (f32[5,64,128]{2,1,0:T(8,128)S(1)}, f32[5,64,128]{2,1,0:T(8,128)S(1)}, f32[5,8,128]{2,1,0:T(8,128)S(1)}) custom-call(f32[5,64,8,128]{3,2,1,0:T(8,128)S(1)} %copy-done), custom_call_target="tpu_custom_call" | custom-call | tf_op jit(solution)/shard_map/edges/pallas_call | solution.py:53
  2.9 3.1 %collective-permute-start.2 = (f32[5,64,128]{2,1,0:T(8,128)S(1)}, f32[5,64,128]{2,1,0:T(8,128)S(1)}, u32[]{:S(2)}, u32[]{:S(2)}) collective-permute-start(f32[5,64,128]{2,1,0:T(8,128)S(1)} %get-tuple-element.8), channel_id=1, source_target_pairs={{0,4},{4,0},{8,12},{12,8},{16,20},{20,16},{24,28},{28,24},{1,5},{5... | collective-permute-start | bytes 491528 | tf_op jit(solution)/shard_map/ppermute | solution.py:450
  5.9 3.5 %collective-permute-start.3 = (f32[5,64,128]{2,1,0:T(8,128)S(1)}, f32[5,64,128]{2,1,0:T(8,128)S(1)}, u32[]{:S(2)}, u32[]{:S(2)}) collective-permute-start(f32[5,64,128]{2,1,0:T(8,128)S(1)} %get-tuple-element.9), channel_id=1, source_target_pairs={{0,28},{4,8},{8,4},{12,16},{16,12},{20,24},{24,20},{28,0},{1,29},{... | collective-permute-start | bytes 491528 | tf_op jit(solution)/shard_map/ppermute | solution.py:450
  9.5 1.6 %collective-permute-start.1 = (f32[5,8,128]{2,1,0:T(8,128)S(1)}, f32[5,8,128]{2,1,0:T(8,128)S(1)}, u32[]{:S(2)}, u32[]{:S(2)}) collective-permute-start(f32[5,8,128]{2,1,0:T(8,128)S(1)} %get-tuple-element.7), channel_id=1, source_target_pairs={{0,3},{1,2},{2,1},{3,0},{4,7},{5,6},{6,5},{7,4},{8,11},{9,10},{10,... | collective-permute-start | bytes 61448 | tf_op jit(solution)/shard_map/ppermute | solution.py:450
  11.1 6.0 %relayout.1.cells_ref = bf16[16,256,1024]{2,1,0:T(8,128)(2,1)S(1)} custom-call(bf16[255,16,8,128]{3,2,1,0:T(8,128)(2,1)} %older_ref.1), custom_call_target="tpu_custom_call" | custom-call | tf_op jit(solution)/shard_map/relayout/pallas_call | solution.py:237
  17.1 4.5 %gram.1 = (f32[136,128]{1,0:T(8,128)S(1)}, f32[136,128]{1,0:T(8,128)S(1)}) custom-call(bf16[16,256,1024]{2,1,0:T(8,128)(2,1)S(1)} %relayout.1.cells_ref, f32[5,64,8,128]{3,2,1,0:T(8,128)S(1)} %copy-done.1, f32[5,64,8,128]{3,2,1,0:T(8,128)S(1)} %copy-done.2, f32[5,8,128]{2,1,0:T(8,128)S(1)} %collective-permute-done.refs_2_.y_a_ref, ...), custom_call_target="tpu_custom_call" | custom-call | tf_op jit(solution)/shard_map/gram/pallas_call | solution.py:327
  21.7 0.1 collective-permute-start.4
  21.8 1.2 %collective-permute-done.4 = f32[136,128]{1,0:T(8,128)S(1)} collective-permute-done((f32[136,128]{1,0:T(8,128)S(1)}, f32[136,128]{1,0:T(8,128)S(1)}, u32[]{:S(2)}, u32[]{:S(2)}) %collective-permute-start.4) | collective-permute-done | bytes 69664 | tf_op jit(solution)/shard_map/ppermute | solution.py:453
  23.0 0.7 %collective-permute-start.5 = (f32[136,128]{1,0:T(8,128)S(1)}, f32[136,128]{1,0:T(8,128)S(1)}, u32[]{:S(2)}, u32[]{:S(2)}) collective-permute-start(f32[136,128]{1,0:T(8,128)S(1)} %add.21), channel_id=1, source_target_pairs={{0,2},{1,3},{2,0},{3,1},{4,6},{5,7},{6,4},{7,5},{8,10},{9,11},{10,... | collective-permute-start | bytes 208904 | tf_op jit(solution)/shard_map/ppermute | solution.py:453
  23.8 2.8 %collective-permute-start.7 = (f32[136,128]{1,0:T(8,128)S(1)}, f32[136,128]{1,0:T(8,128)S(1)}, u32[]{:S(2)}, u32[]{:S(2)}) collective-permute-start(f32[136,128]{1,0:T(8,128)S(1)} %add.21), channel_id=1, source_target_pairs={{0,6},{1,7},{2,4},{3,5},{4,2},{5,3},{6,0},{7,1},{8,14},{9,15},{10,... | collective-permute-start | bytes 208904 | tf_op jit(solution)/shard_map/ppermute | solution.py:453
  26.6 0.8 %collective-permute-done.5 = f32[136,128]{1,0:T(8,128)S(1)} collective-permute-done((f32[136,128]{1,0:T(8,128)S(1)}, f32[136,128]{1,0:T(8,128)S(1)}, u32[]{:S(2)}, u32[]{:S(2)}) %collective-permute-start.5) | collective-permute-done | bytes 69664 | tf_op jit(solution)/shard_map/ppermute | solution.py:453
  27.4 2.0 %collective-permute-done.6 = f32[136,128]{1,0:T(8,128)S(1)} collective-permute-done((f32[136,128]{1,0:T(8,128)S(1)}, f32[136,128]{1,0:T(8,128)S(1)}, u32[]{:S(2)}, u32[]{:S(2)}) %collective-permute-start.6) | collective-permute-done | bytes 69664 | tf_op jit(solution)/shard_map/ppermute | solution.py:453
  29.4 2.3 %collective-permute-start.10 = (f32[136,128]{1,0:T(8,128)S(1)}, f32[136,128]{1,0:T(8,128)S(1)}, u32[]{:S(2)}, u32[]{:S(2)}) collective-permute-start(f32[136,128]{1,0:T(8,128)S(1)} %add_add_fusion.1), channel_id=1, source_target_pairs={{0,24},{1,25},{2,26},{3,27},{4,28},{5,29},{6,30},{7,31},{8,16},{9,... | collective-permute-start | bytes 208904 | tf_op jit(solution)/shard_map/ppermute | solution.py:453
  31.7 2.1 %collective-permute-start.9 = (f32[136,128]{1,0:T(8,128)S(1)}, f32[136,128]{1,0:T(8,128)S(1)}, u32[]{:S(2)}, u32[]{:S(2)}) collective-permute-start(f32[136,128]{1,0:T(8,128)S(1)} %add_add_fusion.1), channel_id=1, source_target_pairs={{0,16},{1,17},{2,18},{3,19},{4,20},{5,21},{6,22},{7,23},{8,24},{9,... | collective-permute-start | bytes 208904 | tf_op jit(solution)/shard_map/ppermute | solution.py:453
  33.9 2.3 %collective-permute-done.10 = f32[136,128]{1,0:T(8,128)S(1)} collective-permute-done((f32[136,128]{1,0:T(8,128)S(1)}, f32[136,128]{1,0:T(8,128)S(1)}, u32[]{:S(2)}, u32[]{:S(2)}) %collective-permute-start.10) | collective-permute-done | bytes 69664 | tf_op jit(solution)/shard_map/ppermute | solution.py:453
  36.1 1.2 %collective-permute-done.8 = f32[136,128]{1,0:T(8,128)S(1)} collective-permute-done((f32[136,128]{1,0:T(8,128)S(1)}, f32[136,128]{1,0:T(8,128)S(1)}, u32[]{:S(2)}, u32[]{:S(2)}) %collective-permute-start.8) | collective-permute-done | bytes 69664 | tf_op jit(solution)/shard_map/ppermute | solution.py:453
  37.3 0.1 collective-permute-start.11
  37.4 1.3 %shard_map.50.refs_6_ = f32[5,64,8,128]{3,2,1,0:T(8,128)} custom-call(f32[5,64,8,128]{3,2,1,0:T(8,128)S(1)} %copy-done.1, f32[5,64,8,128]{3,2,1,0:T(8,128)S(1)} %copy-done.2, f32[5,8,128]{2,1,0:T(8,128)S(1)} %collective-permute-done.refs_2_.y_a_ref, f32[5,8,128]{2,1,0:T(8,128)S(1)} %collective-permute-done.1.refs_3_.y_b_ref, ...), custom_call_target="tpu_custom_call" | custom-call | tf_op jit(solution)/shard_map/pallas_call | solution.py:200
  38.8 1.3 %shard_map.51.refs_6_ = f32[5,64,8,128]{3,2,1,0:T(8,128)} custom-call(f32[5,64,8,128]{3,2,1,0:T(8,128)S(1)} %copy-done.1, f32[5,64,8,128]{3,2,1,0:T(8,128)S(1)} %copy-done.2, f32[5,8,128]{2,1,0:T(8,128)S(1)} %collective-permute-done.refs_2_.y_a_ref, f32[5,8,128]{2,1,0:T(8,128)S(1)} %collective-permute-done.1.refs_3_.y_b_ref, ...), custom_call_target="tpu_custom_call", output_to_operand_aliasing={{}: (6, {})} | custom-call | tf_op jit(solution)/shard_map/pallas_call | solution.py:200
  40.0 1.3 %shard_map.52.refs_6_ = f32[5,64,8,128]{3,2,1,0:T(8,128)} custom-call(f32[5,64,8,128]{3,2,1,0:T(8,128)S(1)} %copy-done.1, f32[5,64,8,128]{3,2,1,0:T(8,128)S(1)} %copy-done.2, f32[5,8,128]{2,1,0:T(8,128)S(1)} %collective-permute-done.refs_2_.y_a_ref, f32[5,8,128]{2,1,0:T(8,128)S(1)} %collective-permute-done.1.refs_3_.y_b_ref, ...), custom_call_target="tpu_custom_call", output_to_operand_aliasing={{}: (6, {})} | custom-call | tf_op jit(solution)/shard_map/pallas_call | solution.py:200
  41.3 1.3 %shard_map.53 = f32[5,64,8,128]{3,2,1,0:T(8,128)} custom-call(f32[5,64,8,128]{3,2,1,0:T(8,128)S(1)} %copy-done.1, f32[5,64,8,128]{3,2,1,0:T(8,128)S(1)} %copy-done.2, f32[5,8,128]{2,1,0:T(8,128)S(1)} %collective-permute-done.refs_2_.y_a_ref, f32[5,8,128]{2,1,0:T(8,128)S(1)} %collective-permute-done.1.refs_3_.y_b_ref, ...), custom_call_target="tpu_custom_call", output_to_operand_aliasing={{}: (6, {})} | custom-call | tf_op jit(solution)/shard_map/pallas_call | solution.py:200
  42.6 8.6 %factor.1 = f32[256,256]{1,0:T(8,128)} custom-call(f32[136,128]{1,0:T(8,128)S(1)} %add_add_fusion.mine_ref, f32[136,128]{1,0:T(8,128)S(1)} %collective-permute-done.11.other_ref), custom_call_target="tpu_custom_call" | custom-call | tf_op jit(solution)/shard_map/factor/pallas_call | solution.py:419
  (17 shorter events, 0.1 us)
Async XLA Ops:
  0.6 1.3 %copy-start = (f32[5,64,8,128]{3,2,1,0:T(8,128)S(1)}, f32[5,64,8,128]{3,2,1,0:T(8,128)}, u32[]{:S(2)}) copy-start(f32[5,64,8,128]{3,2,1,0:T(8,128)} %now_ref.3) | copy-start | bytes 3932164
  2.9 14.2 %collective-permute-start.2 = (f32[5,64,128]{2,1,0:T(8,128)S(1)}, f32[5,64,128]{2,1,0:T(8,128)S(1)}, u32[]{:S(2)}, u32[]{:S(2)}) collective-permute-start(f32[5,64,128]{2,1,0:T(8,128)S(1)} %get-tuple-element.8), channel_id=1, source_target_pairs={{0,4},{4,0},{8,12},{12,8},{16,20},{20,16},{24,28},{28,24},{1,5},{5... | collective-permute-start | bytes 491528 | tf_op jit(solution)/shard_map/ppermute | solution.py:450
  5.9 11.2 %collective-permute-start.3 = (f32[5,64,128]{2,1,0:T(8,128)S(1)}, f32[5,64,128]{2,1,0:T(8,128)S(1)}, u32[]{:S(2)}, u32[]{:S(2)}) collective-permute-start(f32[5,64,128]{2,1,0:T(8,128)S(1)} %get-tuple-element.9), channel_id=1, source_target_pairs={{0,28},{4,8},{8,4},{12,16},{16,12},{20,24},{24,20},{28,0},{1,29},{... | collective-permute-start | bytes 491528 | tf_op jit(solution)/shard_map/ppermute | solution.py:450
  9.5 7.6 %copy-start.1 = (f32[5,64,8,128]{3,2,1,0:T(8,128)S(1)}, f32[5,64,8,128]{3,2,1,0:T(8,128)}, u32[]{:S(2)}) copy-start(f32[5,64,8,128]{3,2,1,0:T(8,128)} %now_ref.3) | copy-start | bytes 3932164
  9.5 7.6 %copy-start.2 = (f32[5,64,8,128]{3,2,1,0:T(8,128)S(1)}, f32[5,64,8,128]{3,2,1,0:T(8,128)}, u32[]{:S(2)}) copy-start(f32[5,64,8,128]{3,2,1,0:T(8,128)} %start_ref.1) | copy-start | bytes 3932164
  9.5 7.6 %collective-permute-start = (f32[5,8,128]{2,1,0:T(8,128)S(1)}, f32[5,8,128]{2,1,0:T(8,128)S(1)}, u32[]{:S(2)}, u32[]{:S(2)}) collective-permute-start(f32[5,8,128]{2,1,0:T(8,128)S(1)} %get-tuple-element.7), channel_id=1, source_target_pairs={{0,1},{1,0},{2,3},{3,2},{4,5},{5,4},{6,7},{7,6},{8,9},{9,8},{10,11... | collective-permute-start | bytes 61448 | tf_op jit(solution)/shard_map/ppermute | solution.py:450
  9.5 7.6 %collective-permute-start.1 = (f32[5,8,128]{2,1,0:T(8,128)S(1)}, f32[5,8,128]{2,1,0:T(8,128)S(1)}, u32[]{:S(2)}, u32[]{:S(2)}) collective-permute-start(f32[5,8,128]{2,1,0:T(8,128)S(1)} %get-tuple-element.7), channel_id=1, source_target_pairs={{0,3},{1,2},{2,1},{3,0},{4,7},{5,6},{6,5},{7,4},{8,11},{9,10},{10,... | collective-permute-start | bytes 61448 | tf_op jit(solution)/shard_map/ppermute | solution.py:450
  21.7 1.3 %collective-permute-start.4 = (f32[136,128]{1,0:T(8,128)S(1)}, f32[136,128]{1,0:T(8,128)S(1)}, u32[]{:S(2)}, u32[]{:S(2)}) collective-permute-start(f32[136,128]{1,0:T(8,128)S(1)} %get-tuple-element.11), channel_id=1, source_target_pairs={{0,1},{1,0},{2,3},{3,2},{4,5},{5,4},{6,7},{7,6},{8,9},{9,8},{10,11... | collective-permute-start | bytes 208904 | tf_op jit(solution)/shard_map/ppermute | solution.py:453
  23.0 4.4 %collective-permute-start.5 = (f32[136,128]{1,0:T(8,128)S(1)}, f32[136,128]{1,0:T(8,128)S(1)}, u32[]{:S(2)}, u32[]{:S(2)}) collective-permute-start(f32[136,128]{1,0:T(8,128)S(1)} %add.21), channel_id=1, source_target_pairs={{0,2},{1,3},{2,0},{3,1},{4,6},{5,7},{6,4},{7,5},{8,10},{9,11},{10,... | collective-permute-start | bytes 208904 | tf_op jit(solution)/shard_map/ppermute | solution.py:453
  23.8 5.6 %collective-permute-start.6 = (f32[136,128]{1,0:T(8,128)S(1)}, f32[136,128]{1,0:T(8,128)S(1)}, u32[]{:S(2)}, u32[]{:S(2)}) collective-permute-start(f32[136,128]{1,0:T(8,128)S(1)} %add.21), channel_id=1, source_target_pairs={{0,4},{1,5},{2,6},{3,7},{4,0},{5,1},{6,2},{7,3},{8,12},{9,13},{10,... | collective-permute-start | bytes 208904 | tf_op jit(solution)/shard_map/ppermute | solution.py:453
  23.8 5.6 %collective-permute-start.7 = (f32[136,128]{1,0:T(8,128)S(1)}, f32[136,128]{1,0:T(8,128)S(1)}, u32[]{:S(2)}, u32[]{:S(2)}) collective-permute-start(f32[136,128]{1,0:T(8,128)S(1)} %add.21), channel_id=1, source_target_pairs={{0,6},{1,7},{2,4},{3,5},{4,2},{5,3},{6,0},{7,1},{8,14},{9,15},{10,... | collective-permute-start | bytes 208904 | tf_op jit(solution)/shard_map/ppermute | solution.py:453
  29.4 6.7 %collective-permute-start.10 = (f32[136,128]{1,0:T(8,128)S(1)}, f32[136,128]{1,0:T(8,128)S(1)}, u32[]{:S(2)}, u32[]{:S(2)}) collective-permute-start(f32[136,128]{1,0:T(8,128)S(1)} %add_add_fusion.1), channel_id=1, source_target_pairs={{0,24},{1,25},{2,26},{3,27},{4,28},{5,29},{6,30},{7,31},{8,16},{9,... | collective-permute-start | bytes 208904 | tf_op jit(solution)/shard_map/ppermute | solution.py:453
  31.7 5.6 %collective-permute-start.8 = (f32[136,128]{1,0:T(8,128)S(1)}, f32[136,128]{1,0:T(8,128)S(1)}, u32[]{:S(2)}, u32[]{:S(2)}) collective-permute-start(f32[136,128]{1,0:T(8,128)S(1)} %add_add_fusion.1), channel_id=1, source_target_pairs={{0,8},{1,9},{2,10},{3,11},{4,12},{5,13},{6,14},{7,15},{8,0},{9,1},... | collective-permute-start | bytes 208904 | tf_op jit(solution)/shard_map/ppermute | solution.py:453
  31.7 5.6 %collective-permute-start.9 = (f32[136,128]{1,0:T(8,128)S(1)}, f32[136,128]{1,0:T(8,128)S(1)}, u32[]{:S(2)}, u32[]{:S(2)}) collective-permute-start(f32[136,128]{1,0:T(8,128)S(1)} %add_add_fusion.1), channel_id=1, source_target_pairs={{0,16},{1,17},{2,18},{3,19},{4,20},{5,21},{6,22},{7,23},{8,24},{9,... | collective-permute-start | bytes 208904 | tf_op jit(solution)/shard_map/ppermute | solution.py:453
  37.3 5.3 %collective-permute-start.11 = (f32[136,128]{1,0:T(8,128)S(1)}, f32[136,128]{1,0:T(8,128)S(1)}, u32[]{:S(2)}, u32[]{:S(2)}) collective-permute-start(f32[136,128]{1,0:T(8,128)S(1)} %add_add_fusion.mine_ref), channel_id=1, source_target_pairs={{0,1},{1,0},{2,3},{3,2},{4,5},{5,4},{6,7},{7,6},{8,9},{9,8},{10,11... | collective-permute-start | bytes 208904 | tf_op jit(solution)/shard_map/ppermute | solution.py:453

commit v5 on v4

--- a/solution.py
+++ b/solution.py
@@ -16,7 +16,6 @@
 PIECES = 4
 IN_VMEM = pl.BlockSpec(memory_space=pltpu.VMEM)
 ROOM = pltpu.CompilerParams(vmem_limit_bytes=20 * 1024 * 1024)
-SPREAD = pltpu.CompilerParams(vmem_limit_bytes=20 * 1024 * 1024)
 
 
 def iota(shape, dim):
@@ -28,22 +27,22 @@
 
 
 def edges_body(now_ref, first_ref, second_ref, cols_ref):
-    fields, planes, rows, lanes = now_ref.shape
+    planes, rows, lanes = now_ref.shape
+    f = pl.program_id(0)
     even = is_even("gx")
-    lo, hi = now_ref[:, :, 0, :], now_ref[:, :, rows - 1, :]
-    first_ref[...] = jnp.where(even, hi, lo)
-    second_ref[...] = jnp.where(even, lo, hi)
+    lo, hi = now_ref[:, 0, :], now_ref[:, rows - 1, :]
+    first_ref[f] = jnp.where(even, hi, lo)
+    second_ref[f] = jnp.where(even, lo, hi)
     key = lax.rem((iota((rows, lanes), 1) + 1) // 2, planes)
     masks = 8
-    for f in range(fields):
-        parts = [jnp.zeros((rows, lanes), jnp.float32)] * masks
-        for z in range(planes):
-            cells = now_ref[f, z]
-            rolled = pltpu.roll(cells, 2 * z, 1) if z else cells
-            parts[z % masks] = jnp.where(key == z, rolled, parts[z % masks])
-        while len(parts) > 1:
-            parts = [x + y for x, y in zip(parts[::2], parts[1::2])]
-        cols_ref[f] = parts[0]
+    parts = [jnp.zeros((rows, lanes), jnp.float32)] * masks
+    for z in range(planes):
+        cells = now_ref[z]
+        rolled = pltpu.roll(cells, 2 * z, 1) if z else cells
+        parts[z % masks] = jnp.where(key == z, rolled, parts[z % masks])
+    while len(parts) > 1:
+        parts = [x + y for x, y in zip(parts[::2], parts[1::2])]
+    cols_ref[f] = parts[0]
 
 
 def edges(now):
@@ -53,7 +52,8 @@
     return pl.pallas_call(
         edges_body,
         out_shape=(line, line, jax.ShapeDtypeStruct((fields, rows, lanes), now.dtype)),
-        in_specs=[IN_VMEM],
+        grid=(fields,),
+        in_specs=[pl.BlockSpec((None, planes, rows, lanes), lambda f: (f, 0, 0, 0))],
         out_specs=(IN_VMEM, IN_VMEM, IN_VMEM),
         compiler_params=ROOM,
         name="edges",
@@ -336,7 +336,7 @@
             pltpu.VMEM((fields, rows, lanes), jnp.float32),
             pltpu.VMEM((2 * size, half), jnp.float32),
         ],
-        compiler_params=SPREAD,
+        compiler_params=ROOM,
         name="gram",
     )(cells, now, start, *around)
 
@@ -442,7 +442,7 @@
 def local(section_start, section_now, history):
     axes = ("gx", "gy")
     count = lax.axis_size("gx") * lax.axis_size("gy")
-    first, second, cols = edges(section_now)
+    first, second, cols = edges(pltpu.with_memory_space_constraint(section_now, pltpu.HBM))
 
     def neighbours(part, axis, by):
         size = lax.axis_size(axis)

time: 51.4 us -> 52.6 us (1.023)
  Pallas kernels: 25.3 us -> 27.7 us
  local copies, waits for them, and re-layouts: 1.32 us -> 0.01 us
    pallas_call x1, Pallas kernels: 0.93 us -> 3.39 us  [edges(): pl.pallas_call(edges_body, out_shape=(line, line, jax.ShapeDtypeStruct((f...]
    unnamed x6 -> x4, local copies, waits for them, and re-layouts: 1.32 us -> 0.01 us
  transfers between devices with their start and end apart: 12 -> 12, of which waited for: 5 -> 5; matrix products, arithmetic and copies ran while one was open for 0% -> 0% of each run, Pallas kernels for 22% -> 21%
where the time goes in v5:
time: 52.6 us; the launch traced here: 52.4 us
  Pallas kernels  27.7 us (53%)
  starting transfers between devices  16.4 us (31%)
  waiting for transfers between devices  7.53 us (14%)
  between operations  0.74 us (1%)
    pallas_call x1, Pallas kernels, factor(): pl.pallas_call(functools.partial(factor_body, 1.0 / rows_total, axis), ou...  8.6 us
    ppermute x4, starting transfers between devices, neighbours(): lax.ppermute(part, axis, [(i, (i + by * (-1) ** i) % size) for i in range...  8.21 us
    ppermute x8, starting transfers between devices, swap(): return lax.ppermute(part, axes, [(i, i ^ bit) for i in range(count)])  8.15 us
    ppermute x8, waiting for transfers between devices, swap(): return lax.ppermute(part, axes, [(i, i ^ bit) for i in range(count)])  7.52 us
    pallas_call x1, Pallas kernels, relayout(): pl.pallas_call(relayout_body, out_shape=jax.ShapeDtypeStruct((samples, sn...  5.98 us
    pallas_call x4, Pallas kernels, stencil(): pl.pallas_call(functools.partial(stencil_body, first), out_shape=jax.Shap...  5.2 us
    pallas_call x1, Pallas kernels, gram(): pl.pallas_call(functools.partial(gram_body, axis=axis), out_shape=(jax.Sh...  4.53 us
    pallas_call x1, Pallas kernels, edges(): pl.pallas_call(edges_body, out_shape=(line, line, jax.ShapeDtypeStruct((f...  3.39 us
  transfers between devices with their start and end apart: 12, of which 5 were waited for; matrix products, arithmetic and copies ran while one was open for 0% of the time, Pallas kernels for 21%

profile of v5, /device:TPU:0, one launch (start us, length us, event | category | flops | bytes accessed | tf_op | source)
XLA Modules:
  0.0 52.4 jit_solution(1829294653026453682)
XLA Ops:
  0.6 3.4 %edges.1 = (f32[5,64,128]{2,1,0:T(8,128)S(1)}, f32[5,64,128]{2,1,0:T(8,128)S(1)}, f32[5,8,128]{2,1,0:T(8,128)S(1)}) custom-call(f32[5,64,8,128]{3,2,1,0:T(8,128)} %now_ref.3), custom_call_target="tpu_custom_call" | custom-call | tf_op jit(solution)/shard_map/edges/pallas_call | solution.py:52
  4.0 3.1 %collective-permute-start.2 = (f32[5,64,128]{2,1,0:T(8,128)S(1)}, f32[5,64,128]{2,1,0:T(8,128)S(1)}, u32[]{:S(2)}, u32[]{:S(2)}) collective-permute-start(f32[5,64,128]{2,1,0:T(8,128)S(1)} %get-tuple-element.8), channel_id=1, source_target_pairs={{0,4},{4,0},{8,12},{12,8},{16,20},{20,16},{24,28},{28,24},{1,5},{5... | collective-permute-start | bytes 491528 | tf_op jit(solution)/shard_map/ppermute | solution.py:450
  7.1 3.5 %collective-permute-start.3 = (f32[5,64,128]{2,1,0:T(8,128)S(1)}, f32[5,64,128]{2,1,0:T(8,128)S(1)}, u32[]{:S(2)}, u32[]{:S(2)}) collective-permute-start(f32[5,64,128]{2,1,0:T(8,128)S(1)} %get-tuple-element.9), channel_id=1, source_target_pairs={{0,28},{4,8},{8,4},{12,16},{16,12},{20,24},{24,20},{28,0},{1,29},{... | collective-permute-start | bytes 491528 | tf_op jit(solution)/shard_map/ppermute | solution.py:450
  10.6 1.6 %collective-permute-start.1 = (f32[5,8,128]{2,1,0:T(8,128)S(1)}, f32[5,8,128]{2,1,0:T(8,128)S(1)}, u32[]{:S(2)}, u32[]{:S(2)}) collective-permute-start(f32[5,8,128]{2,1,0:T(8,128)S(1)} %get-tuple-element.7), channel_id=1, source_target_pairs={{0,3},{1,2},{2,1},{3,0},{4,7},{5,6},{6,5},{7,4},{8,11},{9,10},{10,... | collective-permute-start | bytes 61448 | tf_op jit(solution)/shard_map/ppermute | solution.py:450
  12.2 6.0 %relayout.1.cells_ref = bf16[16,256,1024]{2,1,0:T(8,128)(2,1)S(1)} custom-call(bf16[255,16,8,128]{3,2,1,0:T(8,128)(2,1)} %older_ref.1), custom_call_target="tpu_custom_call" | custom-call | tf_op jit(solution)/shard_map/relayout/pallas_call | solution.py:237
  18.2 0.0 collective-permute-done.1.refs_3_.y_b_ref
  18.3 0.0 collective-permute-done.2.refs_4_.x_a_ref
  18.3 4.5 %gram.1 = (f32[136,128]{1,0:T(8,128)S(1)}, f32[136,128]{1,0:T(8,128)S(1)}) custom-call(bf16[16,256,1024]{2,1,0:T(8,128)(2,1)S(1)} %relayout.1.cells_ref, f32[5,64,8,128]{3,2,1,0:T(8,128)S(1)} %copy-done, f32[5,64,8,128]{3,2,1,0:T(8,128)S(1)} %copy-done.1, f32[5,8,128]{2,1,0:T(8,128)S(1)} %collective-permute-done.refs_2_.y_a_ref, ...), custom_call_target="tpu_custom_call" | custom-call | tf_op jit(solution)/shard_map/gram/pallas_call | solution.py:327
  22.8 0.1 collective-permute-start.4
  22.9 1.2 %collective-permute-done.4 = f32[136,128]{1,0:T(8,128)S(1)} collective-permute-done((f32[136,128]{1,0:T(8,128)S(1)}, f32[136,128]{1,0:T(8,128)S(1)}, u32[]{:S(2)}, u32[]{:S(2)}) %collective-permute-start.4) | collective-permute-done | bytes 69664 | tf_op jit(solution)/shard_map/ppermute | solution.py:453
  24.2 0.7 %collective-permute-start.5 = (f32[136,128]{1,0:T(8,128)S(1)}, f32[136,128]{1,0:T(8,128)S(1)}, u32[]{:S(2)}, u32[]{:S(2)}) collective-permute-start(f32[136,128]{1,0:T(8,128)S(1)} %add.21), channel_id=1, source_target_pairs={{0,2},{1,3},{2,0},{3,1},{4,6},{5,7},{6,4},{7,5},{8,10},{9,11},{10,... | collective-permute-start | bytes 208904 | tf_op jit(solution)/shard_map/ppermute | solution.py:453
  24.9 2.8 %collective-permute-start.7 = (f32[136,128]{1,0:T(8,128)S(1)}, f32[136,128]{1,0:T(8,128)S(1)}, u32[]{:S(2)}, u32[]{:S(2)}) collective-permute-start(f32[136,128]{1,0:T(8,128)S(1)} %add.21), channel_id=1, source_target_pairs={{0,6},{1,7},{2,4},{3,5},{4,2},{5,3},{6,0},{7,1},{8,14},{9,15},{10,... | collective-permute-start | bytes 208904 | tf_op jit(solution)/shard_map/ppermute | solution.py:453
  27.7 0.8 %collective-permute-done.5 = f32[136,128]{1,0:T(8,128)S(1)} collective-permute-done((f32[136,128]{1,0:T(8,128)S(1)}, f32[136,128]{1,0:T(8,128)S(1)}, u32[]{:S(2)}, u32[]{:S(2)}) %collective-permute-start.5) | collective-permute-done | bytes 69664 | tf_op jit(solution)/shard_map/ppermute | solution.py:453
  28.5 2.0 %collective-permute-done.6 = f32[136,128]{1,0:T(8,128)S(1)} collective-permute-done((f32[136,128]{1,0:T(8,128)S(1)}, f32[136,128]{1,0:T(8,128)S(1)}, u32[]{:S(2)}, u32[]{:S(2)}) %collective-permute-start.6) | collective-permute-done | bytes 69664 | tf_op jit(solution)/shard_map/ppermute | solution.py:453
  30.5 2.3 %collective-permute-start.10 = (f32[136,128]{1,0:T(8,128)S(1)}, f32[136,128]{1,0:T(8,128)S(1)}, u32[]{:S(2)}, u32[]{:S(2)}) collective-permute-start(f32[136,128]{1,0:T(8,128)S(1)} %add_add_fusion.1), channel_id=1, source_target_pairs={{0,24},{1,25},{2,26},{3,27},{4,28},{5,29},{6,30},{7,31},{8,16},{9,... | collective-permute-start | bytes 208904 | tf_op jit(solution)/shard_map/ppermute | solution.py:453
  32.9 2.1 %collective-permute-start.9 = (f32[136,128]{1,0:T(8,128)S(1)}, f32[136,128]{1,0:T(8,128)S(1)}, u32[]{:S(2)}, u32[]{:S(2)}) collective-permute-start(f32[136,128]{1,0:T(8,128)S(1)} %add_add_fusion.1), channel_id=1, source_target_pairs={{0,16},{1,17},{2,18},{3,19},{4,20},{5,21},{6,22},{7,23},{8,24},{9,... | collective-permute-start | bytes 208904 | tf_op jit(solution)/shard_map/ppermute | solution.py:453
  35.0 2.3 %collective-permute-done.10 = f32[136,128]{1,0:T(8,128)S(1)} collective-permute-done((f32[136,128]{1,0:T(8,128)S(1)}, f32[136,128]{1,0:T(8,128)S(1)}, u32[]{:S(2)}, u32[]{:S(2)}) %collective-permute-start.10) | collective-permute-done | bytes 69664 | tf_op jit(solution)/shard_map/ppermute | solution.py:453
  37.3 1.2 %collective-permute-done.8 = f32[136,128]{1,0:T(8,128)S(1)} collective-permute-done((f32[136,128]{1,0:T(8,128)S(1)}, f32[136,128]{1,0:T(8,128)S(1)}, u32[]{:S(2)}, u32[]{:S(2)}) %collective-permute-start.8) | collective-permute-done | bytes 69664 | tf_op jit(solution)/shard_map/ppermute | solution.py:453
  38.5 0.1 collective-permute-start.11
  38.6 1.3 %shard_map.50.refs_6_ = f32[5,64,8,128]{3,2,1,0:T(8,128)} custom-call(f32[5,64,8,128]{3,2,1,0:T(8,128)S(1)} %copy-done, f32[5,64,8,128]{3,2,1,0:T(8,128)S(1)} %copy-done.1, f32[5,8,128]{2,1,0:T(8,128)S(1)} %collective-permute-done.refs_2_.y_a_ref, f32[5,8,128]{2,1,0:T(8,128)S(1)} %collective-permute-done.1.refs_3_.y_b_ref, ...), custom_call_target="tpu_custom_call" | custom-call | tf_op jit(solution)/shard_map/pallas_call | solution.py:200
  39.9 1.3 %shard_map.51.refs_6_ = f32[5,64,8,128]{3,2,1,0:T(8,128)} custom-call(f32[5,64,8,128]{3,2,1,0:T(8,128)S(1)} %copy-done, f32[5,64,8,128]{3,2,1,0:T(8,128)S(1)} %copy-done.1, f32[5,8,128]{2,1,0:T(8,128)S(1)} %collective-permute-done.refs_2_.y_a_ref, f32[5,8,128]{2,1,0:T(8,128)S(1)} %collective-permute-done.1.refs_3_.y_b_ref, ...), custom_call_target="tpu_custom_call", output_to_operand_aliasing={{}: (6, {})} | custom-call | tf_op jit(solution)/shard_map/pallas_call | solution.py:200
  41.2 1.3 %shard_map.52.refs_6_ = f32[5,64,8,128]{3,2,1,0:T(8,128)} custom-call(f32[5,64,8,128]{3,2,1,0:T(8,128)S(1)} %copy-done, f32[5,64,8,128]{3,2,1,0:T(8,128)S(1)} %copy-done.1, f32[5,8,128]{2,1,0:T(8,128)S(1)} %collective-permute-done.refs_2_.y_a_ref, f32[5,8,128]{2,1,0:T(8,128)S(1)} %collective-permute-done.1.refs_3_.y_b_ref, ...), custom_call_target="tpu_custom_call", output_to_operand_aliasing={{}: (6, {})} | custom-call | tf_op jit(solution)/shard_map/pallas_call | solution.py:200
  42.5 1.3 %shard_map.53 = f32[5,64,8,128]{3,2,1,0:T(8,128)} custom-call(f32[5,64,8,128]{3,2,1,0:T(8,128)S(1)} %copy-done, f32[5,64,8,128]{3,2,1,0:T(8,128)S(1)} %copy-done.1, f32[5,8,128]{2,1,0:T(8,128)S(1)} %collective-permute-done.refs_2_.y_a_ref, f32[5,8,128]{2,1,0:T(8,128)S(1)} %collective-permute-done.1.refs_3_.y_b_ref, ...), custom_call_target="tpu_custom_call", output_to_operand_aliasing={{}: (6, {})} | custom-call | tf_op jit(solution)/shard_map/pallas_call | solution.py:200
  43.8 8.6 %factor.1 = f32[256,256]{1,0:T(8,128)} custom-call(f32[136,128]{1,0:T(8,128)S(1)} %add_add_fusion.mine_ref, f32[136,128]{1,0:T(8,128)S(1)} %collective-permute-done.11.other_ref), custom_call_target="tpu_custom_call" | custom-call | tf_op jit(solution)/shard_map/factor/pallas_call | solution.py:419
  (15 shorter events, 0.1 us)
Async XLA Ops:
  4.0 14.2 %collective-permute-start.2 = (f32[5,64,128]{2,1,0:T(8,128)S(1)}, f32[5,64,128]{2,1,0:T(8,128)S(1)}, u32[]{:S(2)}, u32[]{:S(2)}) collective-permute-start(f32[5,64,128]{2,1,0:T(8,128)S(1)} %get-tuple-element.8), channel_id=1, source_target_pairs={{0,4},{4,0},{8,12},{12,8},{16,20},{20,16},{24,28},{28,24},{1,5},{5... | collective-permute-start | bytes 491528 | tf_op jit(solution)/shard_map/ppermute | solution.py:450
  7.1 11.2 %collective-permute-start.3 = (f32[5,64,128]{2,1,0:T(8,128)S(1)}, f32[5,64,128]{2,1,0:T(8,128)S(1)}, u32[]{:S(2)}, u32[]{:S(2)}) collective-permute-start(f32[5,64,128]{2,1,0:T(8,128)S(1)} %get-tuple-element.9), channel_id=1, source_target_pairs={{0,28},{4,8},{8,4},{12,16},{16,12},{20,24},{24,20},{28,0},{1,29},{... | collective-permute-start | bytes 491528 | tf_op jit(solution)/shard_map/ppermute | solution.py:450
  10.6 7.6 %copy-start = (f32[5,64,8,128]{3,2,1,0:T(8,128)S(1)}, f32[5,64,8,128]{3,2,1,0:T(8,128)}, u32[]{:S(2)}) copy-start(f32[5,64,8,128]{3,2,1,0:T(8,128)} %now_ref.3) | copy-start | bytes 3932164
  10.6 7.6 %copy-start.1 = (f32[5,64,8,128]{3,2,1,0:T(8,128)S(1)}, f32[5,64,8,128]{3,2,1,0:T(8,128)}, u32[]{:S(2)}) copy-start(f32[5,64,8,128]{3,2,1,0:T(8,128)} %start_ref.1) | copy-start | bytes 3932164
  10.6 7.6 %collective-permute-start = (f32[5,8,128]{2,1,0:T(8,128)S(1)}, f32[5,8,128]{2,1,0:T(8,128)S(1)}, u32[]{:S(2)}, u32[]{:S(2)}) collective-permute-start(f32[5,8,128]{2,1,0:T(8,128)S(1)} %get-tuple-element.7), channel_id=1, source_target_pairs={{0,1},{1,0},{2,3},{3,2},{4,5},{5,4},{6,7},{7,6},{8,9},{9,8},{10,11... | collective-permute-start | bytes 61448 | tf_op jit(solution)/shard_map/ppermute | solution.py:450
  10.6 7.6 %collective-permute-start.1 = (f32[5,8,128]{2,1,0:T(8,128)S(1)}, f32[5,8,128]{2,1,0:T(8,128)S(1)}, u32[]{:S(2)}, u32[]{:S(2)}) collective-permute-start(f32[5,8,128]{2,1,0:T(8,128)S(1)} %get-tuple-element.7), channel_id=1, source_target_pairs={{0,3},{1,2},{2,1},{3,0},{4,7},{5,6},{6,5},{7,4},{8,11},{9,10},{10,... | collective-permute-start | bytes 61448 | tf_op jit(solution)/shard_map/ppermute | solution.py:450
  22.8 1.3 %collective-permute-start.4 = (f32[136,128]{1,0:T(8,128)S(1)}, f32[136,128]{1,0:T(8,128)S(1)}, u32[]{:S(2)}, u32[]{:S(2)}) collective-permute-start(f32[136,128]{1,0:T(8,128)S(1)} %get-tuple-element.11), channel_id=1, source_target_pairs={{0,1},{1,0},{2,3},{3,2},{4,5},{5,4},{6,7},{7,6},{8,9},{9,8},{10,11... | collective-permute-start | bytes 208904 | tf_op jit(solution)/shard_map/ppermute | solution.py:453
  24.2 4.4 %collective-permute-start.5 = (f32[136,128]{1,0:T(8,128)S(1)}, f32[136,128]{1,0:T(8,128)S(1)}, u32[]{:S(2)}, u32[]{:S(2)}) collective-permute-start(f32[136,128]{1,0:T(8,128)S(1)} %add.21), channel_id=1, source_target_pairs={{0,2},{1,3},{2,0},{3,1},{4,6},{5,7},{6,4},{7,5},{8,10},{9,11},{10,... | collective-permute-start | bytes 208904 | tf_op jit(solution)/shard_map/ppermute | solution.py:453
  24.9 5.6 %collective-permute-start.6 = (f32[136,128]{1,0:T(8,128)S(1)}, f32[136,128]{1,0:T(8,128)S(1)}, u32[]{:S(2)}, u32[]{:S(2)}) collective-permute-start(f32[136,128]{1,0:T(8,128)S(1)} %add.21), channel_id=1, source_target_pairs={{0,4},{1,5},{2,6},{3,7},{4,0},{5,1},{6,2},{7,3},{8,12},{9,13},{10,... | collective-permute-start | bytes 208904 | tf_op jit(solution)/shard_map/ppermute | solution.py:453
  24.9 5.6 %collective-permute-start.7 = (f32[136,128]{1,0:T(8,128)S(1)}, f32[136,128]{1,0:T(8,128)S(1)}, u32[]{:S(2)}, u32[]{:S(2)}) collective-permute-start(f32[136,128]{1,0:T(8,128)S(1)} %add.21), channel_id=1, source_target_pairs={{0,6},{1,7},{2,4},{3,5},{4,2},{5,3},{6,0},{7,1},{8,14},{9,15},{10,... | collective-permute-start | bytes 208904 | tf_op jit(solution)/shard_map/ppermute | solution.py:453
  30.5 6.7 %collective-permute-start.10 = (f32[136,128]{1,0:T(8,128)S(1)}, f32[136,128]{1,0:T(8,128)S(1)}, u32[]{:S(2)}, u32[]{:S(2)}) collective-permute-start(f32[136,128]{1,0:T(8,128)S(1)} %add_add_fusion.1), channel_id=1, source_target_pairs={{0,24},{1,25},{2,26},{3,27},{4,28},{5,29},{6,30},{7,31},{8,16},{9,... | collective-permute-start | bytes 208904 | tf_op jit(solution)/shard_map/ppermute | solution.py:453
  32.9 5.6 %collective-permute-start.8 = (f32[136,128]{1,0:T(8,128)S(1)}, f32[136,128]{1,0:T(8,128)S(1)}, u32[]{:S(2)}, u32[]{:S(2)}) collective-permute-start(f32[136,128]{1,0:T(8,128)S(1)} %add_add_fusion.1), channel_id=1, source_target_pairs={{0,8},{1,9},{2,10},{3,11},{4,12},{5,13},{6,14},{7,15},{8,0},{9,1},... | collective-permute-start | bytes 208904 | tf_op jit(solution)/shard_map/ppermute | solution.py:453
  32.9 5.6 %collective-permute-start.9 = (f32[136,128]{1,0:T(8,128)S(1)}, f32[136,128]{1,0:T(8,128)S(1)}, u32[]{:S(2)}, u32[]{:S(2)}) collective-permute-start(f32[136,128]{1,0:T(8,128)S(1)} %add_add_fusion.1), channel_id=1, source_target_pairs={{0,16},{1,17},{2,18},{3,19},{4,20},{5,21},{6,22},{7,23},{8,24},{9,... | collective-permute-start | bytes 208904 | tf_op jit(solution)/shard_map/ppermute | solution.py:453
  38.5 5.3 %collective-permute-start.11 = (f32[136,128]{1,0:T(8,128)S(1)}, f32[136,128]{1,0:T(8,128)S(1)}, u32[]{:S(2)}, u32[]{:S(2)}) collective-permute-start(f32[136,128]{1,0:T(8,128)S(1)} %add_add_fusion.mine_ref), channel_id=1, source_target_pairs={{0,1},{1,0},{2,3},{3,2},{4,5},{5,4},{6,7},{7,6},{8,9},{9,8},{10,11... | collective-permute-start | bytes 208904 | tf_op jit(solution)/shard_map/ppermute | solution.py:453
